TPU v7x, 768 devices: a whole 4x8x12 slice. The times are simulated.
768 devices in a mesh: polar: 8 (over x, y_lo), azimuth: 96 (over z, y_hi, core).
Axes of the slice: x: 4, y: 8 (y_hi: 4, y_lo: 2; y = y_hi * 2 + y_lo), z: 12, core: 2. Of those that a mesh axis runs over, the one named last changes fastest.
Arguments:
- state: float32 [2, 64, 72, 1440], P(None, 'polar', None, 'azimuth'), may hold values from -6 to 6
- kernels: float32 [9, 3, 9, 72], replicated, may hold values from -1.25 to 1.25
- kernel_index: int32 [32], replicated, may hold values from 0 to 8
- w_mix: float32 [72, 641], replicated, may hold values from -0.75 to 0.75
- w_in: float32 [641, 1282], replicated, may hold values from -0.25 to 0.25
- b_in: float32 [1282], replicated, may hold values from -4 to 4
- w_out: float32 [1282, 641], replicated, may hold values from -0.15625 to 0.15625
Outputs:
- encoded: float32 [2, 32, 1440, 641], P(None, 'polar', 'azimuth')
All inputs are finite; a program needn't handle non-finite values.
Results may differ from a plain program's by a relative error of at most 0.000065.
Values sent between devices are 32-bit elements; how exact they have to be, the bound alone decides.
No kernel may reach another device: no remote copies, remote signals or barrier semaphores. Data moves between devices by JAX's collectives and lax.ppermute only.
A program may use at most 32 MiB of HBM per device.

v0:
```python
import jax
import jax.numpy as jnp
from jax import lax
from jax.sharding import PartitionSpec as P

TAPS = 9
SPACING = 90


def shifted(array, axis, by):
    peers = lax.axis_size(axis)
    pairs = [(i, i + by) for i in range(peers) if 0 <= i + by < peers]
    return lax.ppermute(array, axis, pairs)


def row_taps(kernels, kernel_index, out_lat, tap_pos, channel, valid):
    fields = kernels.shape[3]
    total_out = kernel_index.shape[0]
    pick = (out_lat[:, None] == jnp.arange(total_out, dtype=jnp.int32)[None, :]).astype(jnp.int32)
    kernel_of = jnp.sum(pick * kernel_index[None, :], axis=1)
    one_kernel = (
        kernel_of[:, None] == jnp.arange(kernels.shape[0], dtype=jnp.int32)[None, :]
    ).astype(jnp.float32)
    one_tap = (tap_pos[:, None] == jnp.arange(3, dtype=jnp.int32)[None, :]).astype(jnp.float32)
    one_field = (channel[:, None] == jnp.arange(fields, dtype=jnp.int32)[None, :]).astype(
        jnp.float32
    )
    chosen = jnp.einsum(
        "rk,ra,rc,katc->rt",
        one_kernel,
        one_tap,
        one_field,
        kernels,
        precision=lax.Precision.HIGHEST,
        preferred_element_type=jnp.float32,
    )
    return chosen * valid[:, None]


def correlate(cycle, weights):
    half = TAPS // 2
    total = jnp.zeros(cycle.shape, jnp.float32)
    for tap in range(TAPS):
        total = total + weights[:, tap : tap + 1] * jnp.roll(cycle, -(tap - half) * SPACING, axis=1)
    return total


def finish(summed, w_mix, w_in, b_in, w_out):
    lat_half, fields, lon_dev = summed.shape
    mixed = jnp.einsum(
        "ocl,ce->ole",
        summed,
        w_mix,
        precision=lax.Precision.HIGHEST,
        preferred_element_type=jnp.float32,
    ).reshape(lat_half * lon_dev, -1)
    pre = (
        jnp.dot(mixed, w_in, precision=lax.Precision.HIGHEST, preferred_element_type=jnp.float32)
        + b_in
    )
    hidden = jax.nn.gelu(pre, approximate=False)
    out = mixed + jnp.dot(
        hidden, w_out, precision=lax.Precision.HIGHEST, preferred_element_type=jnp.float32
    )
    return out.reshape(lat_half, lon_dev, -1)


def per_device(state, kernels, kernel_index, w_mix, w_in, b_in, w_out):
    members, lat_dev, fields, lon_dev = state.shape
    lat_half = lat_dev // 2
    azim = lax.axis_index("azimuth")
    band = lax.axis_index("polar")
    total_out = kernel_index.shape[0]
    results = []
    for member in range(members):
        block = state[member]
        flat = block.reshape(lat_dev * fields, lon_dev)
        cycle = lax.all_to_all(flat, "azimuth", split_axis=0, concat_axis=1, tiled=True)
        rows_here = cycle.shape[0]
        index = azim * rows_here + jnp.arange(rows_here, dtype=jnp.int32)
        glob = band * lat_dev + index // fields
        channel = index % fields
        parity = glob % 2
        first_w = row_taps(
            kernels,
            kernel_index,
            glob // 2,
            1 + parity,
            channel,
            jnp.ones((rows_here,), jnp.float32),
        )
        second_out = (glob + 1) // 2
        second_ok = ((parity == 1) & (second_out < total_out)).astype(jnp.float32)
        second_w = row_taps(
            kernels, kernel_index, second_out, jnp.zeros_like(glob), channel, second_ok
        )
        planes = jnp.stack([correlate(cycle, first_w), correlate(cycle, second_w)])
        back = lax.all_to_all(planes, "azimuth", split_axis=2, concat_axis=1, tiled=True)
        back = back.reshape(2, lat_half, 2, fields, lon_dev)
        near = back[0, :, 0] + back[0, :, 1]
        upper = back[1, :, 1]
        edge = shifted(upper[-1], "polar", 1)
        summed = near + jnp.concatenate([edge[None], upper[:-1]], axis=0)
        results.append(finish(summed, w_mix, w_in, b_in, w_out))
    return jnp.stack(results)


def solution(mesh):
    placed = (P(None, "polar", None, "azimuth"), P(), P(), P(), P(), P(), P())
    return jax.shard_map(
        per_device,
        mesh=mesh,
        in_specs=placed,
        out_specs=P(None, "polar", "azimuth", None),
        check_vma=False,
    )
```

profile of v0, /device:TPU:1, one launch (start us, length us, event | category | flops | bytes accessed | tf_op | source)
XLA Modules:
  0.0 155.3 jit_solution(13470726512859051412)
XLA Ops:
  0.0 0.9 fusion.262
  0.9 0.2 copy.57
  1.1 0.8 all_to_all.54
  1.9 22.8 %all-to-all-start = ((f32[96,6,15]{2,1,0:T(8,128)}), f32[96,6,15]{2,1,0:T(8,128)S(1)}, u32[]{:S(2)}, u32[]{:S(2)}) async-start(f32[96,6,15]{2,1,0:T(8,128)} %all_to_all.54), calls=%async_computation | async-start | bytes 786432 | tf_op jit(solution)/shard_map/all_to_all | solution.py:78
  24.8 0.9 select_reduce_fusion.1
  25.9 2.0 %convolution_bitcast_fusion.1 = f32[6,9,9]{2,0,1:T(8,128)S(1)} fusion(f32[9,3,9,72]{3,1,2,0:T(4,128)} %param.8, f32[6,3]{0,1:T(4,128)S(1)} %fusion.197, f32[6,72]{1,0:T(8,128)S(1)} %fusion.195), kind=kOutput, calls=%fused_computation.5 | convolution fusion | flops 1261008 | bytes 73728 | tf_op jit(solution)/shard_map/rk,ra,rc,katc->rt/dot_general | solution.py:28
  27.9 0.2 fusion.182
  28.2 2.0 %convolution_bitcast_fusion = f32[6,9,9]{2,0,1:T(8,128)S(1)} fusion(f32[9,3,9,72]{3,1,2,0:T(4,128)} %param.8, f32[3]{0:T(128)S(1)} %compare_convert_fusion, f32[6,72]{1,0:T(8,128)S(1)} %fusion.195), kind=kOutput, calls=%fused_computation.4 | convolution fusion | flops 1261008 | bytes 73668 | tf_op jit(solution)/shard_map/rk,ra,rc,katc->rt/dot_general | solution.py:28
  30.2 0.2 fusion.180
  30.5 0.2 copy.68
  30.6 0.8 all_to_all.62
  31.4 17.2 %all-to-all-done = f32[96,6,15]{2,1,0:T(8,128)S(1)} async-done(((f32[96,6,15]{2,1,0:T(8,128)}), f32[96,6,15]{2,1,0:T(8,128)S(1)}, u32[]{:S(2)}, u32[]{:S(2)}) %all-to-all-start) | async-done | bytes 34592 | tf_op jit(solution)/shard_map/all_to_all | solution.py:78
  48.6 6.6 %all-to-all-start.2 = ((f32[96,6,15]{2,1,0:T(8,128)}), f32[96,6,15]{2,1,0:T(8,128)S(1)}, u32[]{:S(2)}, u32[]{:S(2)}) async-start(f32[96,6,15]{2,1,0:T(8,128)} %all_to_all.62), calls=%async_computation.2 | async-start | bytes 786432 | tf_op jit(solution)/shard_map/all_to_all | solution.py:78
  55.3 0.2 all_to_all.57
  56.1 0.2 all_to_all.58
  56.3 23.0 %all-to-all-done.2 = f32[96,6,15]{2,1,0:T(8,128)S(1)} async-done(((f32[96,6,15]{2,1,0:T(8,128)}), f32[96,6,15]{2,1,0:T(8,128)S(1)}, u32[]{:S(2)}, u32[]{:S(2)}) %all-to-all-start.2) | async-done | bytes 34592 | tf_op jit(solution)/shard_map/all_to_all | solution.py:78
  79.3 0.2 all_to_all.65
  79.5 0.2 all_to_all.66
  80.3 0.1 multiply_add_fusion.2
  80.5 0.1 multiply_add_fusion.3
  80.9 1.5 copy.71
  82.5 2.1 %reshape.2186 = f32[96,1,180]{2,1,0:T(1,128)} reshape(f32[1440,2,6]{2,1,0:T(2,128)S(1)} %bitcast.167) | data formatting | bytes 138240
  84.5 6.5 %all-to-all-start.3 = ((f32[96,1,180]{2,1,0:T(1,128)}), f32[96,1,180]{2,1,0:T(1,128)S(1)}, u32[]{:S(2)}, u32[]{:S(2)}) async-start(f32[96,1,180]{2,1,0:T(1,128)} %reshape.2186), calls=%async_computation.3 | async-start | bytes 196608 | tf_op jit(solution)/shard_map/all_to_all | solution.py:98
  91.1 1.5 copy.61
  92.6 2.0 %reshape.2188 = f32[96,1,180]{2,1,0:T(1,128)} reshape(f32[1440,2,6]{2,1,0:T(2,128)S(1)} %bitcast.168) | data formatting | bytes 138240
  94.7 12.6 %all-to-all-done.3 = f32[96,1,180]{2,1,0:T(1,128)S(1)} async-done(((f32[96,1,180]{2,1,0:T(1,128)}), f32[96,1,180]{2,1,0:T(1,128)S(1)}, u32[]{:S(2)}, u32[]{:S(2)}) %all-to-all-start.3) | async-done | bytes 69152 | tf_op jit(solution)/shard_map/all_to_all | solution.py:98
  107.3 5.5 %all-to-all-start.1 = ((f32[96,1,180]{2,1,0:T(1,128)}), f32[96,1,180]{2,1,0:T(1,128)S(1)}, u32[]{:S(2)}, u32[]{:S(2)}) async-start(f32[96,1,180]{2,1,0:T(1,128)} %reshape.2188), calls=%async_computation.1 | async-start | bytes 196608 | tf_op jit(solution)/shard_map/all_to_all | solution.py:98
  112.8 0.5 broadcast.1212
  113.3 0.9 reduce
  114.2 1.0 reshape.2187
  115.2 2.0 %copy.88 = f32[2,6,96,15]{3,2,0,1:T(8,128)S(1)} copy(f32[2,6,96,15]{1,0,3,2:T(2,128)S(1)} %bitcast.169) | data formatting | bytes 138240 | tf_op jit(solution)/shard_map/all_to_all | solution.py:98
  117.2 0.5 copy.73
  117.7 2.3 %collective-permute-start.1 = (f32[72,15]{1,0:T(8,128)S(1)}, f32[72,15]{1,0:T(8,128)S(1)}, u32[]{:S(2)}, u32[]{:S(2)}) collective-permute-start(f32[72,15]{1,0:T(8,128)S(1)} %bitcast.189), channel_id=1, source_target_pairs={{0,96},{96,192},{192,288},{288,384},{384,480},{480,576},{576,672},... | collective-permute-start | bytes 12968 | tf_op jit(solution)/shard_map/ppermute | solution.py:13
  120.0 0.2 fusion.261
  120.2 8.7 %all-to-all-done.1 = f32[96,1,180]{2,1,0:T(1,128)S(1)} async-done(((f32[96,1,180]{2,1,0:T(1,128)}), f32[96,1,180]{2,1,0:T(1,128)S(1)}, u32[]{:S(2)}, u32[]{:S(2)}) %all-to-all-start.1) | async-done | bytes 69152 | tf_op jit(solution)/shard_map/all_to_all | solution.py:98
  129.0 0.9 reduce.1
  129.9 1.0 reshape.2189
  130.9 2.0 %copy.87 = f32[2,6,96,15]{3,2,0,1:T(8,128)S(1)} copy(f32[2,6,96,15]{1,0,3,2:T(2,128)S(1)} %bitcast.170) | data formatting | bytes 138240 | tf_op jit(solution)/shard_map/all_to_all | solution.py:98
  132.9 0.5 copy.63
  133.4 0.2 fusion.260
  133.9 2.3 %collective-permute-start = (f32[72,15]{1,0:T(8,128)S(1)}, f32[72,15]{1,0:T(8,128)S(1)}, u32[]{:S(2)}, u32[]{:S(2)}) collective-permute-start(f32[72,15]{1,0:T(8,128)S(1)} %bitcast.190), channel_id=1, source_target_pairs={{0,96},{96,192},{192,288},{288,384},{384,480},{480,576},{576,672},... | collective-permute-start | bytes 12968 | tf_op jit(solution)/shard_map/ppermute | solution.py:13
  136.4 0.3 fusion.264
  136.7 4.3 %convolution_add_fusion = f32[60,1282]{1,0:T(8,128)S(1)} fusion(f32[60,641]{1,0:T(8,128)S(1)} %fusion.264, f32[641,1282]{1,0:T(8,128)} %param.11, f32[1282]{0:T(1024)S(1)} %copy-done.1), kind=kOutput, calls=%fused_computation | convolution fusion | flops 591745536 | bytes 3753696 | tf_op jit(solution)/shard_map/dot_general | solution.py:58
  141.0 4.2 %convolution_add_fusion.2 = f32[60,641]{1,0:T(8,128)S(1)} fusion(f32[60,641]{1,0:T(8,128)S(1)} %fusion.264, f32[1282,641]{0,1:T(8,128)S(1)} %copy-done.2, f32[60,1282]{1,0:T(8,128)S(1)} %convolution_add_fusion), kind=kOutput, calls=%fused_computation.2 | convolution fusion | flops 596629952 | bytes 3902408 | tf_op jit(solution)/shard_map/dot_general | solution.py:62
  145.4 0.3 fusion.263
  145.7 4.3 %convolution_add_fusion.1 = f32[60,1282]{1,0:T(8,128)S(1)} fusion(f32[60,641]{1,0:T(8,128)S(1)} %fusion.263, f32[641,1282]{1,0:T(8,128)} %param.11, f32[1282]{0:T(1024)S(1)} %copy-done.1), kind=kOutput, calls=%fused_computation.1 | convolution fusion | flops 591745536 | bytes 3753696 | tf_op jit(solution)/shard_map/dot_general | solution.py:58
  150.0 4.2 %convolution_add_fusion.3 = f32[60,641]{1,0:T(8,128)S(1)} fusion(f32[60,641]{1,0:T(8,128)S(1)} %fusion.263, f32[1282,641]{0,1:T(8,128)S(1)} %copy-done.3, f32[60,1282]{1,0:T(8,128)S(1)} %convolution_add_fusion.1), kind=kOutput, calls=%fused_computation.3 | convolution fusion | flops 596629952 | bytes 3902408 | tf_op jit(solution)/shard_map/dot_general | solution.py:62
  154.3 1.0 copy.78
  (58 shorter events, 2.8 us)
Async XLA Ops:
  0.0 136.3 %copy-start = (f32[72,641]{1,0:T(8,128)S(1)}, f32[72,641]{1,0:T(8,128)}, u32[]{:S(2)}) copy-start(f32[72,641]{1,0:T(8,128)} %param.10) | copy-start | bytes 553828
  1.9 46.7 %all-to-all-start = ((f32[96,6,15]{2,1,0:T(8,128)}), f32[96,6,15]{2,1,0:T(8,128)S(1)}, u32[]{:S(2)}, u32[]{:S(2)}) async-start(f32[96,6,15]{2,1,0:T(8,128)} %all_to_all.54), calls=%async_computation | async-start | bytes 786432 | tf_op jit(solution)/shard_map/all_to_all | solution.py:78
  48.6 30.7 %all-to-all-start.2 = ((f32[96,6,15]{2,1,0:T(8,128)}), f32[96,6,15]{2,1,0:T(8,128)S(1)}, u32[]{:S(2)}, u32[]{:S(2)}) async-start(f32[96,6,15]{2,1,0:T(8,128)} %all_to_all.62), calls=%async_computation.2 | async-start | bytes 786432 | tf_op jit(solution)/shard_map/all_to_all | solution.py:78
  84.5 22.7 %all-to-all-start.3 = ((f32[96,1,180]{2,1,0:T(1,128)}), f32[96,1,180]{2,1,0:T(1,128)S(1)}, u32[]{:S(2)}, u32[]{:S(2)}) async-start(f32[96,1,180]{2,1,0:T(1,128)} %reshape.2186), calls=%async_computation.3 | async-start | bytes 196608 | tf_op jit(solution)/shard_map/all_to_all | solution.py:98
  107.3 21.7 %all-to-all-start.1 = ((f32[96,1,180]{2,1,0:T(1,128)}), f32[96,1,180]{2,1,0:T(1,128)S(1)}, u32[]{:S(2)}, u32[]{:S(2)}) async-start(f32[96,1,180]{2,1,0:T(1,128)} %reshape.2188), calls=%async_computation.1 | async-start | bytes 196608 | tf_op jit(solution)/shard_map/all_to_all | solution.py:98
  117.7 18.5 %collective-permute-start.1 = (f32[72,15]{1,0:T(8,128)S(1)}, f32[72,15]{1,0:T(8,128)S(1)}, u32[]{:S(2)}, u32[]{:S(2)}) collective-permute-start(f32[72,15]{1,0:T(8,128)S(1)} %bitcast.189), channel_id=1, source_target_pairs={{0,96},{96,192},{192,288},{288,384},{384,480},{480,576},{576,672},... | collective-permute-start | bytes 12968 | tf_op jit(solution)/shard_map/ppermute | solution.py:13
  129.9 6.8 %copy-start.1 = (f32[1282]{0:T(1024)S(1)}, f32[1282]{0:T(1024)}, u32[]{:S(2)}) copy-start(f32[1282]{0:T(1024)} %param.12) | copy-start | bytes 15388
  133.9 11.4 %collective-permute-start = (f32[72,15]{1,0:T(8,128)S(1)}, f32[72,15]{1,0:T(8,128)S(1)}, u32[]{:S(2)}, u32[]{:S(2)}) collective-permute-start(f32[72,15]{1,0:T(8,128)S(1)} %bitcast.190), channel_id=1, source_target_pairs={{0,96},{96,192},{192,288},{288,384},{384,480},{480,576},{576,672},... | collective-permute-start | bytes 12968 | tf_op jit(solution)/shard_map/ppermute | solution.py:13
  136.3 4.6 %copy-start.2 = (f32[1282,641]{0,1:T(8,128)S(1)}, f32[1282,641]{0,1:T(8,128)}, u32[]{:S(2)}) copy-start(f32[1282,641]{0,1:T(8,128)} %param.13) | copy-start | bytes 9861148
  145.4 4.6 %copy-start.3 = (f32[1282,641]{0,1:T(8,128)S(1)}, f32[1282,641]{0,1:T(8,128)}, u32[]{:S(2)}) copy-start(f32[1282,641]{0,1:T(8,128)} %param.13) | copy-start | bytes 9861148
where the time goes:
time: 156 us; the launch traced here: 155 us
  waiting for transfers between devices  61.5 us (39%)
  starting transfers between devices  46.1 us (30%)
  matrix products  21.9 us (14%)
  local copies, waits for them, and re-layouts  21.6 us (14%)
  other arithmetic  3.61 us (2%)
    all_to_all x2, waiting for transfers between devices, per_device(): lax.all_to_all(flat, 'azimuth', split_axis=0, concat_axis=1, tiled=True)  40.1 us
    all_to_all x2, starting transfers between devices, per_device(): lax.all_to_all(flat, 'azimuth', split_axis=0, concat_axis=1, tiled=True)  29.5 us
    all_to_all x2, waiting for transfers between devices, per_device(): lax.all_to_all(planes, 'azimuth', split_axis=2, concat_axis=1, tiled=True)  21.3 us
    all_to_all x2, starting transfers between devices, per_device(): lax.all_to_all(planes, 'azimuth', split_axis=2, concat_axis=1, tiled=True)  12.1 us
    dot_general x2, matrix products, finish(): jnp.dot(mixed, w_in, precision=lax.Precision.HIGHEST, preferred_element_t...  8.56 us
    dot_general x2, matrix products, finish(): jnp.dot(hidden, w_out, precision=lax.Precision.HIGHEST, preferred_element...  8.42 us
    unnamed x12, local copies, waits for them, and re-layouts  6.11 us
    all_to_all x5, local copies, waits for them, and re-layouts, per_device(): lax.all_to_all(planes, 'azimuth', split_axis=2, concat_axis=1, tiled=True)  5.43 us
  transfers between devices with their start and end apart: 6, of which 4 were waited for; matrix products, arithmetic and copies ran while one was open for 19% of the time, Pallas kernels for 0%

commit v1 on v0

v1 whole, which is shorter than its diff:
```python
import functools

import jax
import jax.numpy as jnp
from jax import lax
from jax.experimental import pallas as pl
from jax.experimental.pallas import tpu as pltpu
from jax.sharding import PartitionSpec as P

SPACING = 90
VMEM = pl.BlockSpec(memory_space=pltpu.VMEM)
SMEM = pl.BlockSpec(memory_space=pltpu.SMEM)
ANY = pl.BlockSpec(memory_space=pl.ANY)
BF16 = jnp.bfloat16
F32 = jnp.float32


def ring(array, by):
    peers = lax.axis_size("azimuth")
    return lax.ppermute(array, "azimuth", [(i, (i + by) % peers) for i in range(peers)])


def next_band(array):
    peers = lax.axis_size("polar")
    return lax.ppermute(array, "polar", [(i, i + 1) for i in range(peers - 1)])


def near(array):
    return pltpu.with_memory_space_constraint(array, pltpu.VMEM)


def halves(a):
    high = a.astype(BF16)
    return high, (a - high.astype(F32)).astype(BF16)


def dot(a, b):
    return jnp.dot(a, b, preferred_element_type=F32)


def dot_t(a, b):
    return lax.dot_general(a, b, (((1,), (1,)), ((), ())), preferred_element_type=F32)


def taps_kernel(index_ref, band_ref, kern_ref, near_ref, upper_ref):
    taps, lat, _ = near_ref.shape
    outs = lat // 2
    last = index_ref.shape[0] - 1
    first = band_ref[0] * outs
    upper_ref[...] = jnp.zeros(upper_ref.shape, F32)
    for o in range(outs):
        here = index_ref[first + o]
        after = index_ref[jnp.minimum(first + o + 1, last)]
        for t in range(taps):
            near_ref[t, 2 * o : 2 * o + 2, :] = kern_ref[here, t, 1:3, :]
            upper_ref[t, 2 * o + 1 : 2 * o + 2, :] = kern_ref[after, t, 0:1, :]


def partial_kernel(x_ref, left_ref, right_ref, near_ref, upper_ref, _, *rest):
    outs, (near_s, upper_s) = rest[:3], rest[3:]
    members, lons, lat, fields = x_ref.shape
    count = members * lons
    half = lat // 2
    upper_s[0:lat, :] = jnp.zeros((lat, upper_s.shape[1]), F32)
    for s in range(3):
        base = 3 * s
        for m in range(members):
            for n in range(lons):
                i = m * lons + n
                three = (left_ref[m, n], x_ref[m, n], right_ref[m, n])
                near = three[0] * near_ref[base]
                upper = three[0] * upper_ref[base]
                for u in (1, 2):
                    near = near + three[u] * near_ref[base + u]
                    upper = upper + three[u] * upper_ref[base + u]
                near_s[i * lat : (i + 1) * lat, 0:fields] = near
                upper_s[(i + 1) * lat : (i + 2) * lat, 0:fields] = upper
        rows = count * half
        even = near_s[pl.ds(0, rows, stride=2), :]
        odd = near_s[pl.ds(1, rows, stride=2), :]
        above = upper_s[pl.ds(lat - 1, rows, stride=2), :]
        place = lax.broadcasted_iota(jnp.int32, above.shape, 0)
        above = jnp.where(place % half == 0, 0.0, above)
        outs[s][0:rows, :] = (even + odd + above)[:, 0:fields]
        halo = upper_s[pl.ds(2 * lat - 1, count, stride=lat), :]
        outs[s][rows : rows + count, :] = halo[:, 0:fields]


def in_kernel(mix_ref, in_ref, mix_h, mix_l, in_h, in_l):
    mh, ml = halves(mix_ref[...])
    wh, wl = halves(in_ref[...])
    both = dot(mh, wh) + dot(ml, wh) + dot(mh, wl)
    mix_h[...], mix_l[...] = mh, ml
    in_h[...], in_l[...] = halves(both)


def out_kernel(out_ref, out_h, out_l):
    out_h[...], out_l[...] = halves(out_ref[...])


def halo_kernel(z_ref, a_ref, b_ref, _, halo_ref):
    rows = z_ref.shape[0] - halo_ref.shape[0]
    halo_ref[...] = z_ref[rows:, :] + a_ref[rows:, :] + b_ref[rows:, :]


def fetch(pairs, sems):
    copies = [pltpu.make_async_copy(src, dst, sems.at[i]) for i, (src, dst) in enumerate(pairs)]
    for copy in copies:
        copy.start()
    return copies


def mlp(corr, mix_h, mix_l, in_h, in_l, b_in, out_h, out_l, copies):
    ch, cl = halves(corr)
    pre = dot(ch, in_h[...]) + dot(cl, in_h[...]) + dot(ch, in_l[...]) + b_in[...]
    hidden = 0.5 * pre * (1.0 + lax.erf(pre * 0.7071067811865476))
    hh, hl = halves(hidden)
    mixed = dot(ch, mix_h[...]) + dot(cl, mix_h[...]) + dot(ch, mix_l[...])
    copies[0].wait()
    total = mixed + (dot_t(hh, out_h[...]) + dot_t(hl, out_h[...]))
    copies[1].wait()
    return total + dot_t(hh, out_l[...])


def main_kernel(z_ref, a_ref, b_ref, *rest):
    weights, (oh, ol, res_ref, out_h, out_l, sems) = rest[:5], rest[5:]
    copies = fetch(((oh, out_h), (ol, out_l)), sems)
    rows = res_ref.shape[0]
    corr = z_ref[0:rows, :] + a_ref[0:rows, :] + b_ref[0:rows, :]
    res_ref[...] = mlp(corr, *weights, out_h, out_l, copies)


def edge_kernel(half, z_ref, a_ref, b_ref, halo_ref, res_ref, *rest):
    weights, (oh, ol, out_ref, scratch, out_h, out_l, sems) = rest[:5], rest[5:]
    copies = fetch(((oh, out_h), (ol, out_l)), sems)
    count = halo_ref.shape[0]
    fields = halo_ref.shape[1]
    total = z_ref[...] + a_ref[...] + b_ref[...]
    scratch[:, 0:fields] = total
    corr = scratch[pl.ds(0, count, stride=half), :][:, 0:fields] + halo_ref[...]
    members, lons = out_ref.shape[:2]
    for m in range(members):
        for n in range(lons):
            i = m * lons + n
            out_ref[m, n] = res_ref[half * i : half * (i + 1), :]
    fixed = mlp(corr, *weights, out_h, out_l, copies)
    for m in range(members):
        for n in range(lons):
            i = m * lons + n
            out_ref[m, n, 0:1, :] = fixed[i : i + 1, :]


def per_device(state, kernels, kernel_index, w_mix, w_in, b_in, w_out):
    members, lat, fields, lons = state.shape
    half = lat // 2
    count = members * lons
    rows = count * half
    taps = kernels.shape[2]
    embed, ffn = w_in.shape
    step = SPACING // lons
    S, V = jax.ShapeDtypeStruct, pltpu.VMEM

    x = jnp.transpose(state, (0, 3, 1, 2))
    left = ring(x, step)
    right = ring(x, -step)

    band = lax.axis_index("polar").astype(jnp.int32).reshape(1)
    nearby, upper = pl.pallas_call(
        taps_kernel,
        out_shape=[V((taps, lat, fields), F32)] * 2,
        in_specs=[SMEM, SMEM, VMEM],
        out_specs=[VMEM] * 2,
        name="taps",
    )(kernel_index, band, jnp.transpose(kernels, (0, 2, 1, 3)))
    mix_h, mix_l, in_h, in_l = pl.pallas_call(
        in_kernel,
        out_shape=[V((fields, embed), BF16)] * 2 + [V((fields, ffn), BF16)] * 2,
        in_specs=[VMEM] * 2,
        out_specs=[VMEM] * 4,
        name="w_in",
    )(w_mix, w_in)
    out_h, out_l = pl.pallas_call(
        out_kernel,
        out_shape=[S((embed, ffn), BF16)] * 2,
        in_specs=[VMEM],
        out_specs=[VMEM] * 2,
        name="w_out",
    )(jnp.transpose(w_out))
    bias = b_in.reshape(1, ffn)

    low, mid, high = pl.pallas_call(
        partial_kernel,
        out_shape=[V((rows + count, fields), F32)] * 3,
        in_specs=[VMEM] * 5 + [ANY],
        out_specs=[VMEM] * 3,
        scratch_shapes=[pltpu.VMEM((count * lat, 128), F32), pltpu.VMEM(((count + 1) * lat, 128), F32)],
        name="partial",
    )(x, near(left), near(right), near(nearby), near(upper), near(mix_l))
    from_high = near(ring(high, -3 * step))
    from_low = near(ring(low, 3 * step))
    mid = near(mid)

    packed = tuple(near(a) for a in (mix_h, mix_l, in_h, in_l, bias)) + (out_h, out_l)
    fetched = [pltpu.VMEM((embed, ffn), BF16)] * 2 + [pltpu.SemaphoreType.DMA((2,))]
    halo = pl.pallas_call(
        halo_kernel,
        out_shape=V((count, fields), F32),
        in_specs=[VMEM] * 3 + [ANY],
        out_specs=VMEM,
        name="halo",
    )(mid, from_high, from_low, out_l)
    halo = next_band(halo)
    res = pl.pallas_call(
        main_kernel,
        out_shape=V((rows, embed), F32),
        in_specs=[VMEM] * 8 + [ANY] * 2,
        out_specs=VMEM,
        scratch_shapes=fetched,
        name="main",
    )(mid, from_high, from_low, *packed)
    out = pl.pallas_call(
        functools.partial(edge_kernel, half),
        out_shape=S((members, lons, half, embed), F32),
        in_specs=[VMEM] * 10 + [ANY] * 2,
        out_specs=VMEM,
        scratch_shapes=[pltpu.VMEM((rows + count, 128), F32)] + fetched,
        name="edge",
    )(mid, from_high, from_low, near(halo), near(res), *packed)
    return jnp.transpose(out, (0, 2, 1, 3))


def solution(mesh):
    placed = (P(None, "polar", None, "azimuth"), P(), P(), P(), P(), P(), P())
    return jax.shard_map(
        per_device,
        mesh=mesh,
        in_specs=placed,
        out_specs=P(None, "polar", "azimuth", None),
        check_vma=False,
    )
```

time: 156 us -> 60.1 us (0.39)
  the two profiles are of different devices: /device:TPU:1 before, /device:TPU:8 now
where the time goes in v1:
time: 60.1 us; the launch traced here: 59.8 us
  starting transfers between devices  34.2 us (57%)
  Pallas kernels  18 us (30%)
  waiting for transfers between devices  7.46 us (12%)
    ppermute x4, starting transfers between devices, ring(): lax.ppermute(array, 'azimuth', [(i, (i + by) % peers) for i in range(peer...  27.1 us
    ppermute x4, waiting for transfers between devices, ring(): lax.ppermute(array, 'azimuth', [(i, (i + by) % peers) for i in range(peer...  7.46 us
    ppermute x1, starting transfers between devices, next_band(): return lax.ppermute(array, 'polar', [(i, i + 1) for i in range(peers - 1)])  7.09 us
    pallas_call x1, Pallas kernels, per_device(): pl.pallas_call(main_kernel, out_shape=V((rows, embed), F32), in_specs=[VM...  4.35 us
    pallas_call x1, Pallas kernels, per_device(): pl.pallas_call(functools.partial(edge_kernel, half), out_shape=S((members...  4.28 us
    pallas_call x1, Pallas kernels, per_device(): pl.pallas_call(out_kernel, out_shape=[S((embed, ffn), BF16)] * 2, in_spec...  4.12 us
    pallas_call x1, Pallas kernels, per_device(): pl.pallas_call(in_kernel, out_shape=[V((fields, embed), BF16)] * 2 + [V((...  3.23 us
  transfers between devices with their start and end apart: 5, of which 2 were waited for; matrix products, arithmetic and copies ran while one was open for 0% of the time, Pallas kernels for 21%

profile of v1, /device:TPU:8, one launch (start us, length us, event | category | flops | bytes accessed | tf_op | source)
XLA Modules:
  0.0 59.8 jit_solution(5542779468569693712)
XLA Ops:
  0.0 16.6 %collective-permute-start.1 = (f32[2,15,8,72]{3,2,1,0:T(8,128)}, f32[2,15,8,72]{3,2,1,0:T(8,128)S(1)}, u32[]{:S(2)}, u32[]{:S(2)}) collective-permute-start(f32[2,15,8,72]{3,2,1,0:T(8,128)} %bitcast.7), channel_id=1, source_target_pairs={{0,90},{1,91},{2,92},{3,93},{4,94},{5,95},{6,0},{7,1},{8,2},{9,3},... | collective-permute-start | bytes 207368 | tf_op jit(solution)/shard_map/ppermute | solution.py:20
  16.6 1.9 %collective-permute-start = (f32[2,15,8,72]{3,2,1,0:T(8,128)}, f32[2,15,8,72]{3,2,1,0:T(8,128)S(1)}, u32[]{:S(2)}, u32[]{:S(2)}) collective-permute-start(f32[2,15,8,72]{3,2,1,0:T(8,128)} %bitcast.8), channel_id=1, source_target_pairs={{0,6},{1,7},{2,8},{3,9},{4,10},{5,11},{6,12},{7,13},{8,14},{9,15},... | collective-permute-start | bytes 207368 | tf_op jit(solution)/shard_map/ppermute | solution.py:20
  18.5 3.2 %w_in.1 = (bf16[72,641]{1,0:T(8,128)(2,1)S(1)}, bf16[72,641]{1,0:T(8,128)(2,1)S(1)}, bf16[72,1282]{1,0:T(8,128)(2,1)S(1)}, bf16[72,1282]{1,0:T(8,128)(2,1)S(1)}) custom-call(f32[72,641]{1,0:T(8,128)} %mix_ref.1, f32[641,1282]{1,0:T(8,128)} %in_ref.1), custom_call_target="tpu_custom_call" | custom-call | tf_op jit(solution)/shard_map/w_in/pallas_call | solution.py:175
  21.8 0.0 copy-start
  21.8 1.0 %taps.1 = (f32[9,8,72]{2,1,0:T(8,128)S(1)}, f32[9,8,72]{2,1,0:T(8,128)S(1)}) custom-call(s32[32]{0:T(128)} %index_ref.1, s32[1]{0:T(128)} %bitcast.1.band_ref, f32[9,9,3,72]{3,2,1,0:T(4,128)} %bitcast.6), custom_call_target="tpu_custom_call" | custom-call | tf_op jit(solution)/shard_map/taps/pallas_call | solution.py:168
  22.8 0.0 collective-permute-done.1.right_ref
  22.8 5.4 %collective-permute-done.left_ref = f32[2,15,8,72]{3,2,1,0:T(8,128)S(1)} collective-permute-done((f32[2,15,8,72]{3,2,1,0:T(8,128)}, f32[2,15,8,72]{3,2,1,0:T(8,128)S(1)}, u32[]{:S(2)}, u32[]{:S(2)}) %collective-permute-start) | collective-permute-done | bytes 69152 | tf_op jit(solution)/shard_map/ppermute | solution.py:20
  28.1 1.1 %partial.1 = (f32[150,72]{1,0:T(8,128)S(1)}, f32[150,72]{1,0:T(8,128)S(1)}, f32[150,72]{1,0:T(8,128)S(1)}) custom-call(f32[2,15,8,72]{3,2,1,0:T(8,128)} %bitcast.9, f32[2,15,8,72]{3,2,1,0:T(8,128)S(1)} %collective-permute-done.left_ref, f32[2,15,8,72]{3,2,1,0:T(8,128)S(1)} %collective-permute-done.1.right_ref, f32[9,8,72]{2,1,0:T(8,128)S(1)} %get-tuple-element.16.near_ref, ...), custom_call_target="tpu_custom_call" | custom-call | tf_op jit(solution)/shard_map/partial/pallas_call | solution.py:191
  29.2 1.9 %collective-permute-start.2 = (f32[150,72]{1,0:T(8,128)S(1)}, f32[150,72]{1,0:T(8,128)S(1)}, u32[]{:S(2)}, u32[]{:S(2)}) collective-permute-start(f32[150,72]{1,0:T(8,128)S(1)} %get-tuple-element.20), channel_id=1, source_target_pairs={{0,78},{1,79},{2,80},{3,81},{4,82},{5,83},{6,84},{7,85},{8,86},{9,... | collective-permute-start | bytes 129608 | tf_op jit(solution)/shard_map/ppermute | solution.py:20
  31.1 6.6 %collective-permute-start.3 = (f32[150,72]{1,0:T(8,128)S(1)}, f32[150,72]{1,0:T(8,128)S(1)}, u32[]{:S(2)}, u32[]{:S(2)}) collective-permute-start(f32[150,72]{1,0:T(8,128)S(1)} %get-tuple-element.21), channel_id=1, source_target_pairs={{0,18},{1,19},{2,20},{3,21},{4,22},{5,23},{6,24},{7,25},{8,26},{9,... | collective-permute-start | bytes 129608 | tf_op jit(solution)/shard_map/ppermute | solution.py:20
  37.8 4.1 %w_out.1 = (bf16[641,1282]{1,0:T(8,128)(2,1)}, bf16[641,1282]{1,0:T(8,128)(2,1)}) custom-call(f32[641,1282]{1,0:T(8,128)} %bitcast.5), custom_call_target="tpu_custom_call" | custom-call | tf_op jit(solution)/shard_map/w_out/pallas_call | solution.py:182
  41.9 0.0 collective-permute-done.2.a_ref
  41.9 2.1 %collective-permute-done.3.b_ref = f32[150,72]{1,0:T(8,128)S(1)} collective-permute-done((f32[150,72]{1,0:T(8,128)S(1)}, f32[150,72]{1,0:T(8,128)S(1)}, u32[]{:S(2)}, u32[]{:S(2)}) %collective-permute-start.3) | collective-permute-done | bytes 43232 | tf_op jit(solution)/shard_map/ppermute | solution.py:20
  44.0 7.1 %collective-permute-start.4 = (f32[30,72]{1,0:T(8,128)S(1)}, f32[30,72]{1,0:T(8,128)S(1)}, u32[]{:S(2)}, u32[]{:S(2)}) collective-permute-start(f32[30,72]{1,0:T(8,128)S(1)} %halo.1), channel_id=1, source_target_pairs={{0,96},{96,192},{192,288},{288,384},{384,480},{480,576},{576,672},... | collective-permute-start | bytes 25928 | tf_op jit(solution)/shard_map/ppermute | solution.py:25
  51.1 0.0 copy-done
  51.1 4.4 %main.1.res_ref = f32[120,641]{1,0:T(8,128)S(1)} custom-call(f32[150,72]{1,0:T(8,128)S(1)} %get-tuple-element.19.z_ref, f32[150,72]{1,0:T(8,128)S(1)} %collective-permute-done.2.a_ref, f32[150,72]{1,0:T(8,128)S(1)} %collective-permute-done.3.b_ref, bf16[72,641]{1,0:T(8,128)(2,1)S(1)} %get-tuple-element.23.rest_0_, ...), custom_call_target="tpu_custom_call" | custom-call | tf_op jit(solution)/shard_map/main/pallas_call | solution.py:213
  55.5 0.0 collective-permute-done.4.halo_ref
  55.5 4.3 %edge.1 = f32[2,15,4,641]{3,2,1,0:T(4,128)} custom-call(f32[150,72]{1,0:T(8,128)S(1)} %get-tuple-element.19.z_ref, f32[150,72]{1,0:T(8,128)S(1)} %collective-permute-done.2.a_ref, f32[150,72]{1,0:T(8,128)S(1)} %collective-permute-done.3.b_ref, f32[30,72]{1,0:T(8,128)S(1)} %collective-permute-done.4.halo_ref, f32[120,641]{1,0:T(8,128)S(1)} %main.1.res_ref, ...), custom_call_target="tpu_custom_call" | custom-call | tf_op jit(solution)/shard_map/edge/pallas_call | solution.py:221
  (2 shorter events, 0.0 us)
Async XLA Ops:
  0.0 22.8 %collective-permute-start.1 = (f32[2,15,8,72]{3,2,1,0:T(8,128)}, f32[2,15,8,72]{3,2,1,0:T(8,128)S(1)}, u32[]{:S(2)}, u32[]{:S(2)}) collective-permute-start(f32[2,15,8,72]{3,2,1,0:T(8,128)} %bitcast.7), channel_id=1, source_target_pairs={{0,90},{1,91},{2,92},{3,93},{4,94},{5,95},{6,0},{7,1},{8,2},{9,3},... | collective-permute-start | bytes 207368 | tf_op jit(solution)/shard_map/ppermute | solution.py:20
  16.6 11.5 %collective-permute-start = (f32[2,15,8,72]{3,2,1,0:T(8,128)}, f32[2,15,8,72]{3,2,1,0:T(8,128)S(1)}, u32[]{:S(2)}, u32[]{:S(2)}) collective-permute-start(f32[2,15,8,72]{3,2,1,0:T(8,128)} %bitcast.8), channel_id=1, source_target_pairs={{0,6},{1,7},{2,8},{3,9},{4,10},{5,11},{6,12},{7,13},{8,14},{9,15},... | collective-permute-start | bytes 207368 | tf_op jit(solution)/shard_map/ppermute | solution.py:20
  21.8 29.3 %copy-start = (f32[1282]{0:T(1024)S(1)}, f32[1282]{0:T(1024)}, u32[]{:S(2)}) copy-start(f32[1282]{0:T(1024)} %param.12) | copy-start | bytes 15388
  29.2 12.7 %collective-permute-start.2 = (f32[150,72]{1,0:T(8,128)S(1)}, f32[150,72]{1,0:T(8,128)S(1)}, u32[]{:S(2)}, u32[]{:S(2)}) collective-permute-start(f32[150,72]{1,0:T(8,128)S(1)} %get-tuple-element.20), channel_id=1, source_target_pairs={{0,78},{1,79},{2,80},{3,81},{4,82},{5,83},{6,84},{7,85},{8,86},{9,... | collective-permute-start | bytes 129608 | tf_op jit(solution)/shard_map/ppermute | solution.py:20
  31.1 12.9 %collective-permute-start.3 = (f32[150,72]{1,0:T(8,128)S(1)}, f32[150,72]{1,0:T(8,128)S(1)}, u32[]{:S(2)}, u32[]{:S(2)}) collective-permute-start(f32[150,72]{1,0:T(8,128)S(1)} %get-tuple-element.21), channel_id=1, source_target_pairs={{0,18},{1,19},{2,20},{3,21},{4,22},{5,23},{6,24},{7,25},{8,26},{9,... | collective-permute-start | bytes 129608 | tf_op jit(solution)/shard_map/ppermute | solution.py:20
  44.0 11.5 %collective-permute-start.4 = (f32[30,72]{1,0:T(8,128)S(1)}, f32[30,72]{1,0:T(8,128)S(1)}, u32[]{:S(2)}, u32[]{:S(2)}) collective-permute-start(f32[30,72]{1,0:T(8,128)S(1)} %halo.1), channel_id=1, source_target_pairs={{0,96},{96,192},{192,288},{288,384},{384,480},{480,576},{576,672},... | collective-permute-start | bytes 25928 | tf_op jit(solution)/shard_map/ppermute | solution.py:25

commit v2 on v1

v2 whole, which is shorter than its diff:
```python
import functools

import jax
import jax.numpy as jnp
from jax import lax
from jax.experimental import pallas as pl
from jax.experimental.pallas import tpu as pltpu
from jax.sharding import PartitionSpec as P


SPACING = 90
LANES = 128
VMEM = pl.BlockSpec(memory_space=pltpu.VMEM)
SMEM = pl.BlockSpec(memory_space=pltpu.SMEM)
ANY = pl.BlockSpec(memory_space=pl.ANY)
BF16 = jnp.bfloat16
F32 = jnp.float32


def ring(array, by):
    peers = lax.axis_size("azimuth")
    return lax.ppermute(array, "azimuth", [(i, (i + by) % peers) for i in range(peers)])


def next_band(array):
    peers = lax.axis_size("polar")
    return lax.ppermute(array, "polar", [(i, i + 1) for i in range(peers - 1)])


def near(array):
    return pltpu.with_memory_space_constraint(array, pltpu.VMEM)


def halves(a):
    high = a.astype(BF16)
    return high, (a - high.astype(F32)).astype(BF16)


def dot(a, b):
    return jnp.dot(a, b, preferred_element_type=F32)


def dot_t(a, b):
    return lax.dot_general(a, b, (((1,), (1,)), ((), ())), preferred_element_type=F32)


def unpack(out, packed, residual, rows):
    members = 2
    lons, group, cut, rest = rows
    pad = out.shape[0] // members
    full = lons * group
    out[...] = jnp.zeros(out.shape, F32)
    out[0:full, 0:cut] = packed[0:full, 0:cut]
    out[pad : pad + full, 0:cut] = packed[0:full, cut : 2 * cut]
    for m in range(members):
        for n in range(lons):
            at = m * pad + n * group
            lane = n * rest
            out[at : at + group, cut : cut + rest] = packed[
                residual + m * group : residual + (m + 1) * group, lane : lane + rest
            ]


def pack_kernel(x_ref, out_ref):
    members, lons, lat, fields = x_ref.shape
    cut = LANES // 2
    rest = fields - cut
    for m in range(members):
        out_ref[lons + m] = jnp.zeros((lat, LANES), F32)
        for n in range(lons):
            tile = x_ref[m, n]
            out_ref[n, :, m * cut : (m + 1) * cut] = tile[:, 0:cut]
            out_ref[lons + m, :, n * rest : (n + 1) * rest] = tile[:, cut:fields]


def taps_kernel(index_ref, band_ref, kern_ref, near_ref, upper_ref, near_s, upper_s):
    taps, lat, fields = near_s.shape
    outs = lat // 2
    cut = LANES // 2
    rest = fields - cut
    last = index_ref.shape[0] - 1
    first = band_ref[0] * outs
    upper_s[...] = jnp.zeros(upper_s.shape, F32)
    for o in range(outs):
        here = index_ref[first + o]
        after = index_ref[jnp.minimum(first + o + 1, last)]
        for t in range(taps):
            near_s[t, 2 * o : 2 * o + 2, :] = kern_ref[here, t, 1:3, :]
            upper_s[t, 2 * o + 1 : 2 * o + 2, :] = kern_ref[after, t, 0:1, :]
    for src, dst in ((near_s, near_ref), (upper_s, upper_ref)):
        for t in range(taps):
            tile = src[t]
            dst[t, 0] = jnp.concatenate([tile[:, 0:cut]] * 2, axis=1)
            dst[t, 1] = jnp.concatenate([tile[:, cut:fields]] * (LANES // rest), axis=1)


def partial_kernel(x_ref, left_ref, right_ref, near_ref, upper_ref, _, *rest):
    outs, (near_s, upper_s) = rest[:3], rest[3:]
    tiles, lat, lanes = x_ref.shape
    half = lat // 2
    pairs = tiles - 2
    rows = tiles * half
    upper_s[0:lat, :] = jnp.zeros((lat, lanes), F32)
    for s in range(3):
        base = 3 * s
        for i in range(tiles):
            kind = int(i >= pairs)
            three = (left_ref[i], x_ref[i], right_ref[i])
            near = three[0] * near_ref[base, kind]
            upper = three[0] * upper_ref[base, kind]
            for u in (1, 2):
                near = near + three[u] * near_ref[base + u, kind]
                upper = upper + three[u] * upper_ref[base + u, kind]
            near_s[i * lat : (i + 1) * lat, :] = near
            upper_s[(i + 1) * lat : (i + 2) * lat, :] = upper
        even = near_s[pl.ds(0, rows, stride=2), :]
        odd = near_s[pl.ds(1, rows, stride=2), :]
        above = upper_s[pl.ds(lat - 1, rows, stride=2), :]
        place = lax.broadcasted_iota(jnp.int32, above.shape, 0)
        above = jnp.where(place % half == 0, 0.0, above)
        outs[s][0:rows, :] = even + odd + above
        outs[s][rows : rows + tiles, :] = upper_s[pl.ds(2 * lat - 1, tiles, stride=lat), :]


def spans(total, size):
    return [(at, min(size, total - at)) for at in range(0, total, size)]


def in_kernel(mix_ref, in_hbm, mix_h, mix_l, in_h, in_l, in_v, sems):
    parts = spans(in_v.shape[0], 128)
    copies = fetch([(in_hbm.at[pl.ds(*p), :], in_v.at[pl.ds(*p), :]) for p in parts], sems)
    mh, ml = halves(mix_ref[...])
    mix_h[...], mix_l[...] = mh, ml
    both = jnp.zeros(in_h.shape, F32)
    for copy, (at, size) in zip(copies, parts):
        copy.wait()
        wh, wl = halves(in_v[at : at + size, :])
        a, b = mh[:, at : at + size], ml[:, at : at + size]
        both = both + (dot(a, wh) + dot(b, wh) + dot(a, wl))
    in_h[...], in_l[...] = halves(both)


def out_kernel(out_hbm, out_h, low_hbm, out_v, low_v, sems, low_sems):
    parts = spans(out_v.shape[0], 112)
    copies = fetch([(out_hbm.at[pl.ds(*p), :], out_v.at[pl.ds(*p), :]) for p in parts], sems)
    stores = [
        pltpu.make_async_copy(low_v.at[pl.ds(*p), :], low_hbm.at[pl.ds(*p), :], low_sems.at[k])
        for k, p in enumerate(parts)
    ]
    for copy, store, (at, size) in zip(copies, stores, parts):
        copy.wait()
        out_h[at : at + size, :], low_v[at : at + size, :] = halves(out_v[at : at + size, :])
        store.start()
    for store in stores:
        store.wait()


def halo_kernel(z_ref, a_ref, b_ref, _, halo_ref):
    rows = z_ref.shape[0] - halo_ref.shape[0]
    halo_ref[...] = z_ref[rows:, :] + a_ref[rows:, :] + b_ref[rows:, :]


def fetch(pairs, sems):
    copies = [pltpu.make_async_copy(src, dst, sems.at[i]) for i, (src, dst) in enumerate(pairs)]
    for copy in copies:
        copy.start()
    return copies


def stacked(a):
    return jnp.concatenate(halves(a), axis=0)


def product(both, weight, contract):
    rows = both.shape[0] // 2
    total = contract(both, weight)
    return total[:rows] + total[rows:]


def mlp(corr_s, fields, weights, low_hbm, low_v, sems, both_s, res_s, prepare):
    mix_h, mix_l, in_h, in_l, b_in, out_h = weights
    copy = fetch(((low_hbm, low_v),), sems)[0]

    @pl.when(lax.axis_index("polar") >= 0)
    def _():
        prepare()
        both = stacked(corr_s[:, 0:fields])
        rows = corr_s.shape[0]
        pre = product(both, in_h[...], dot) + dot(both[:rows], in_l[...]) + b_in[...]
        hidden = 0.5 * pre * (1.0 + lax.erf(pre * 0.7071067811865476))
        both_s[...] = stacked(hidden)
        res_s[...] = product(both, mix_h[...], dot) + dot(both[:rows], mix_l[...])

    rows = corr_s.shape[0]
    both = both_s[...]
    total = res_s[...] + product(both, out_h[...], dot_t)
    copy.wait()
    return total + dot_t(both[:rows], low_v[...])


def main_kernel(fields, shape, z_ref, a_ref, b_ref, *rest):
    weights, (low_hbm, res_ref, sum_s, corr_s, both_s, low_v, sems) = rest[:6], rest[6:]
    lons, half = shape

    def prepare():
        sum_s[...] = z_ref[...] + a_ref[...] + b_ref[...]
        cut = LANES // 2
        unpack(corr_s, sum_s, lons * half, (lons, half, cut, fields - cut))

    res_ref[...] = mlp(corr_s, fields, weights, low_hbm, low_v, sems, both_s, res_ref, prepare)


def edge_kernel(fields, z_ref, a_ref, b_ref, halo_ref, res_ref, *rest):
    weights, (low_hbm, out_ref, sum_s, corr_s, both_s, fixed_s, low_v, sems) = rest[:6], rest[6:]
    members, lons, half, _ = out_ref.shape
    tiles = halo_ref.shape[0]
    pad = res_ref.shape[0] // members

    def prepare():
        sum_s[...] = z_ref[...] + a_ref[...] + b_ref[...]
        ends = sum_s[pl.ds(0, tiles, stride=half), :]
        sum_s[0:tiles, :] = ends + halo_ref[...]
        cut = LANES // 2
        unpack(corr_s, sum_s, lons, (lons, 1, cut, fields - cut))
        for m in range(members):
            for n in range(lons):
                at = m * pad + n * half
                out_ref[m, n] = res_ref[at : at + half, :]

    fixed = mlp(corr_s, fields, weights, low_hbm, low_v, sems, both_s, fixed_s, prepare)
    for m in range(members):
        for n in range(lons):
            at = m * (fixed.shape[0] // members) + n
            out_ref[m, n, 0:1, :] = fixed[at : at + 1, :]


def per_device(state, kernels, kernel_index, w_mix, w_in, b_in, w_out):
    members, lat, fields, lons = state.shape
    half = lat // 2
    tiles = lons + members
    taps = kernels.shape[2]
    embed, ffn = w_in.shape
    step = SPACING // lons
    S, V, DMA = jax.ShapeDtypeStruct, pltpu.VMEM, pltpu.SemaphoreType.DMA

    x = pl.pallas_call(
        pack_kernel,
        out_shape=V((tiles, lat, LANES), F32),
        in_specs=[VMEM],
        out_specs=VMEM,
        name="pack",
    )(jnp.transpose(state, (0, 3, 1, 2)))
    left = ring(x, step)
    right = ring(x, -step)

    band = lax.axis_index("polar").astype(jnp.int32).reshape(1)
    nearby, upper = pl.pallas_call(
        taps_kernel,
        out_shape=[V((taps, 2, lat, LANES), F32)] * 2,
        in_specs=[SMEM, SMEM, VMEM],
        out_specs=[VMEM] * 2,
        scratch_shapes=[V((taps, lat, fields), F32)] * 2,
        name="taps",
    )(kernel_index, band, jnp.transpose(kernels, (0, 2, 1, 3)))
    parts = len(spans(embed, 128))
    mix_h, mix_l, in_h, in_l = pl.pallas_call(
        in_kernel,
        out_shape=[V((fields, embed), BF16)] * 2 + [V((fields, ffn), BF16)] * 2,
        in_specs=[VMEM, ANY],
        out_specs=[VMEM] * 4,
        scratch_shapes=[V((embed, ffn), F32), DMA((parts,))],
        name="w_in",
    )(w_mix, w_in)
    parts = len(spans(embed, 112))
    out_h, out_l = pl.pallas_call(
        out_kernel,
        out_shape=[V((embed, ffn), BF16), S((embed, ffn), BF16)],
        in_specs=[ANY],
        out_specs=[VMEM, ANY],
        scratch_shapes=[V((embed, ffn), F32), V((embed, ffn), BF16), DMA((parts,)), DMA((parts,))],
        name="w_out",
    )(jnp.transpose(w_out))
    bias = b_in.reshape(1, ffn)

    rows = tiles * (half + 1)
    low, mid, high = pl.pallas_call(
        partial_kernel,
        out_shape=[V((rows, LANES), F32)] * 3,
        in_specs=[VMEM] * 5 + [ANY],
        out_specs=[VMEM] * 3,
        scratch_shapes=[V((tiles * lat, LANES), F32), V(((tiles + 1) * lat, LANES), F32)],
        name="partial",
    )(near(x), near(left), near(right), near(nearby), near(upper), near(mix_l))
    from_low = near(ring(low, 3 * step))
    from_high = near(ring(high, -3 * step))
    mid = near(mid)

    packed = tuple(near(a) for a in (mix_h, mix_l, in_h, in_l, bias, out_h)) + (out_l,)
    halo = pl.pallas_call(
        halo_kernel,
        out_shape=V((tiles, LANES), F32),
        in_specs=[VMEM] * 3 + [ANY],
        out_specs=VMEM,
        name="halo",
    )(mid, from_high, from_low, out_l)
    halo = next_band(halo)
    fetched = [V((embed, ffn), BF16), DMA((1,))]
    pad = members * (-(-lons * half // 16) * 16)
    res = pl.pallas_call(
        functools.partial(main_kernel, fields, (lons, half)),
        out_shape=V((pad, embed), F32),
        in_specs=[VMEM] * 9 + [ANY],
        out_specs=VMEM,
        scratch_shapes=[V((rows, LANES), F32), V((pad, LANES), F32), V((2 * pad, ffn), BF16)] + fetched,
        name="main",
    )(mid, from_high, from_low, *packed)
    pad = members * (-(-lons // 16) * 16)
    out = pl.pallas_call(
        functools.partial(edge_kernel, fields),
        out_shape=S((members, lons, half, embed), F32),
        in_specs=[VMEM] * 11 + [ANY],
        out_specs=VMEM,
        scratch_shapes=[V((rows, LANES), F32), V((pad, LANES), F32), V((2 * pad, ffn), BF16), V((pad, embed), F32)]
        + fetched,
        name="edge",
    )(mid, from_high, from_low, near(halo), near(res), *packed)
    return jnp.transpose(out, (0, 2, 1, 3))


def solution(mesh):
    placed = (P(None, "polar", None, "azimuth"), P(), P(), P(), P(), P(), P())
    return jax.shard_map(
        per_device,
        mesh=mesh,
        in_specs=placed,
        out_specs=P(None, "polar", "azimuth", None),
        check_vma=False,
    )
```

time: 60.1 us -> 54.2 us (0.902)
  the two profiles are of different devices: /device:TPU:8 before, /device:TPU:2 now
where the time goes in v2:
time: 54.2 us; the launch traced here: 53.8 us
  starting transfers between devices  29.3 us (54%)
  Pallas kernels  14.1 us (26%)
  waiting for transfers between devices  10.2 us (19%)
    ppermute x4, starting transfers between devices, ring(): lax.ppermute(array, 'azimuth', [(i, (i + by) % peers) for i in range(peer...  27.1 us
    ppermute x4, waiting for transfers between devices, ring(): lax.ppermute(array, 'azimuth', [(i, (i + by) % peers) for i in range(peer...  8.33 us
    pallas_call x1, Pallas kernels, per_device(): pl.pallas_call(in_kernel, out_shape=[V((fields, embed), BF16)] * 2 + [V((...  3.55 us
    pallas_call x1, Pallas kernels, per_device(): pl.pallas_call(functools.partial(edge_kernel, fields), out_shape=S((membe...  3.02 us
    pallas_call x1, Pallas kernels, per_device(): pl.pallas_call(out_kernel, out_shape=[V((embed, ffn), BF16), S((embed, ff...  2.83 us
    pallas_call x1, Pallas kernels, per_device(): pl.pallas_call(functools.partial(main_kernel, fields, (lons, half)), out_...  2.3 us
    ppermute x1, starting transfers between devices, next_band(): return lax.ppermute(array, 'polar', [(i, i + 1) for i in range(peers - 1)])  2.23 us
    ppermute x1, waiting for transfers between devices, next_band(): return lax.ppermute(array, 'polar', [(i, i + 1) for i in range(peers - 1)])  1.9 us
  transfers between devices with their start and end apart: 5, of which 3 were waited for; matrix products, arithmetic and copies ran while one was open for 0% of the time, Pallas kernels for 19%

profile of v2, /device:TPU:2, one launch (start us, length us, event | category | flops | bytes accessed | tf_op | source)
XLA Modules:
  0.0 53.8 jit_solution(1568526881617510570)
XLA Ops:
  0.0 1.0 %pack.1.x_ref = f32[17,8,128]{2,1,0:T(8,128)S(1)} custom-call(f32[2,15,8,72]{3,2,1,0:T(8,128)} %bitcast.7), custom_call_target="tpu_custom_call" | custom-call | tf_op jit(solution)/shard_map/pack/pallas_call | solution.py:246
  1.0 16.6 %collective-permute-start.1 = (f32[17,8,128]{2,1,0:T(8,128)S(1)}, f32[17,8,128]{2,1,0:T(8,128)S(1)}, u32[]{:S(2)}, u32[]{:S(2)}) collective-permute-start(f32[17,8,128]{2,1,0:T(8,128)S(1)} %pack.1.x_ref), channel_id=1, source_target_pairs={{0,90},{1,91},{2,92},{3,93},{4,94},{5,95},{6,0},{7,1},{8,2},{9,3},... | collective-permute-start | bytes 208904 | tf_op jit(solution)/shard_map/ppermute | solution.py:22
  17.6 1.9 %collective-permute-start = (f32[17,8,128]{2,1,0:T(8,128)S(1)}, f32[17,8,128]{2,1,0:T(8,128)S(1)}, u32[]{:S(2)}, u32[]{:S(2)}) collective-permute-start(f32[17,8,128]{2,1,0:T(8,128)S(1)} %pack.1.x_ref), channel_id=1, source_target_pairs={{0,6},{1,7},{2,8},{3,9},{4,10},{5,11},{6,12},{7,13},{8,14},{9,15},... | collective-permute-start | bytes 208904 | tf_op jit(solution)/shard_map/ppermute | solution.py:22
  19.6 3.6 %w_in.1 = (bf16[72,641]{1,0:T(8,128)(2,1)S(1)}, bf16[72,641]{1,0:T(8,128)(2,1)S(1)}, bf16[72,1282]{1,0:T(8,128)(2,1)S(1)}, bf16[72,1282]{1,0:T(8,128)(2,1)S(1)}) custom-call(f32[72,641]{1,0:T(8,128)} %mix_ref.1, f32[641,1282]{1,0:T(8,128)} %in_hbm.1), custom_call_target="tpu_custom_call" | custom-call | tf_op jit(solution)/shard_map/w_in/pallas_call | solution.py:266
  23.1 0.0 copy-start
  23.1 1.3 %taps.1 = (f32[9,2,8,128]{3,2,1,0:T(8,128)S(1)}, f32[9,2,8,128]{3,2,1,0:T(8,128)S(1)}) custom-call(s32[32]{0:T(128)} %index_ref.1, s32[1]{0:T(128)} %bitcast.1.band_ref, f32[9,9,3,72]{3,2,1,0:T(4,128)} %bitcast.6), custom_call_target="tpu_custom_call" | custom-call | tf_op jit(solution)/shard_map/taps/pallas_call | solution.py:257
  24.4 0.0 collective-permute-done.1.right_ref
  24.4 2.7 %collective-permute-done.left_ref = f32[17,8,128]{2,1,0:T(8,128)S(1)} collective-permute-done((f32[17,8,128]{2,1,0:T(8,128)S(1)}, f32[17,8,128]{2,1,0:T(8,128)S(1)}, u32[]{:S(2)}, u32[]{:S(2)}) %collective-permute-start) | collective-permute-done | bytes 69664 | tf_op jit(solution)/shard_map/ppermute | solution.py:22
  27.2 0.1 partial.1
  27.3 4.6 %collective-permute-start.2 = (f32[85,128]{1,0:T(8,128)S(1)}, f32[85,128]{1,0:T(8,128)S(1)}, u32[]{:S(2)}, u32[]{:S(2)}) collective-permute-start(f32[85,128]{1,0:T(8,128)S(1)} %get-tuple-element.20), channel_id=1, source_target_pairs={{0,78},{1,79},{2,80},{3,81},{4,82},{5,83},{6,84},{7,85},{8,86},{9,... | collective-permute-start | bytes 130568 | tf_op jit(solution)/shard_map/ppermute | solution.py:22
  31.9 3.9 %collective-permute-start.3 = (f32[85,128]{1,0:T(8,128)S(1)}, f32[85,128]{1,0:T(8,128)S(1)}, u32[]{:S(2)}, u32[]{:S(2)}) collective-permute-start(f32[85,128]{1,0:T(8,128)S(1)} %get-tuple-element.21), channel_id=1, source_target_pairs={{0,18},{1,19},{2,20},{3,21},{4,22},{5,23},{6,24},{7,25},{8,26},{9,... | collective-permute-start | bytes 130568 | tf_op jit(solution)/shard_map/ppermute | solution.py:22
  35.9 2.8 %w_out.1 = (bf16[641,1282]{1,0:T(8,128)(2,1)S(1)}, bf16[641,1282]{1,0:T(8,128)(2,1)}) custom-call(f32[641,1282]{1,0:T(8,128)} %bitcast.5), custom_call_target="tpu_custom_call" | custom-call | tf_op jit(solution)/shard_map/w_out/pallas_call | solution.py:275
  38.7 0.0 collective-permute-done.2.a_ref
  38.7 5.6 %collective-permute-done.3.b_ref = f32[85,128]{1,0:T(8,128)S(1)} collective-permute-done((f32[85,128]{1,0:T(8,128)S(1)}, f32[85,128]{1,0:T(8,128)S(1)}, u32[]{:S(2)}, u32[]{:S(2)}) %collective-permute-start.3) | collective-permute-done | bytes 43552 | tf_op jit(solution)/shard_map/ppermute | solution.py:22
  44.3 2.2 %collective-permute-start.4 = (f32[17,128]{1,0:T(8,128)S(1)}, f32[17,128]{1,0:T(8,128)S(1)}, u32[]{:S(2)}, u32[]{:S(2)}) collective-permute-start(f32[17,128]{1,0:T(8,128)S(1)} %halo.1), channel_id=1, source_target_pairs={{0,96},{96,192},{192,288},{288,384},{384,480},{480,576},{576,672},... | collective-permute-start | bytes 26120 | tf_op jit(solution)/shard_map/ppermute | solution.py:27
  46.5 0.0 copy-done
  46.6 2.3 %main.1.res_ref = f32[128,641]{1,0:T(8,128)S(1)} custom-call(f32[85,128]{1,0:T(8,128)S(1)} %get-tuple-element.19.z_ref, f32[85,128]{1,0:T(8,128)S(1)} %collective-permute-done.2.a_ref, f32[85,128]{1,0:T(8,128)S(1)} %collective-permute-done.3.b_ref, bf16[72,641]{1,0:T(8,128)(2,1)S(1)} %get-tuple-element.23.rest_0_, ...), custom_call_target="tpu_custom_call" | custom-call | tf_op jit(solution)/shard_map/main/pallas_call | solution.py:309
  48.9 1.9 %collective-permute-done.4.halo_ref = f32[17,128]{1,0:T(8,128)S(1)} collective-permute-done((f32[17,128]{1,0:T(8,128)S(1)}, f32[17,128]{1,0:T(8,128)S(1)}, u32[]{:S(2)}, u32[]{:S(2)}) %collective-permute-start.4) | collective-permute-done | bytes 8736 | tf_op jit(solution)/shard_map/ppermute | solution.py:27
  50.8 3.0 %edge.1 = f32[2,15,4,641]{3,2,1,0:T(4,128)} custom-call(f32[85,128]{1,0:T(8,128)S(1)} %get-tuple-element.19.z_ref, f32[85,128]{1,0:T(8,128)S(1)} %collective-permute-done.2.a_ref, f32[85,128]{1,0:T(8,128)S(1)} %collective-permute-done.3.b_ref, f32[17,128]{1,0:T(8,128)S(1)} %collective-permute-done.4.halo_ref, f32[128,641]{1,0:T(8,128)S(1)} %main.1.res_ref, ...), custom_call_target="tpu_custom_call" | custom-call | tf_op jit(solution)/shard_map/edge/pallas_call | solution.py:318
  (2 shorter events, 0.0 us)
Async XLA Ops:
  1.0 23.4 %collective-permute-start.1 = (f32[17,8,128]{2,1,0:T(8,128)S(1)}, f32[17,8,128]{2,1,0:T(8,128)S(1)}, u32[]{:S(2)}, u32[]{:S(2)}) collective-permute-start(f32[17,8,128]{2,1,0:T(8,128)S(1)} %pack.1.x_ref), channel_id=1, source_target_pairs={{0,90},{1,91},{2,92},{3,93},{4,94},{5,95},{6,0},{7,1},{8,2},{9,3},... | collective-permute-start | bytes 208904 | tf_op jit(solution)/shard_map/ppermute | solution.py:22
  17.6 9.6 %collective-permute-start = (f32[17,8,128]{2,1,0:T(8,128)S(1)}, f32[17,8,128]{2,1,0:T(8,128)S(1)}, u32[]{:S(2)}, u32[]{:S(2)}) collective-permute-start(f32[17,8,128]{2,1,0:T(8,128)S(1)} %pack.1.x_ref), channel_id=1, source_target_pairs={{0,6},{1,7},{2,8},{3,9},{4,10},{5,11},{6,12},{7,13},{8,14},{9,15},... | collective-permute-start | bytes 208904 | tf_op jit(solution)/shard_map/ppermute | solution.py:22
  23.1 23.4 %copy-start = (f32[1282]{0:T(1024)S(1)}, f32[1282]{0:T(1024)}, u32[]{:S(2)}) copy-start(f32[1282]{0:T(1024)} %param.12) | copy-start | bytes 15388
  27.3 11.4 %collective-permute-start.2 = (f32[85,128]{1,0:T(8,128)S(1)}, f32[85,128]{1,0:T(8,128)S(1)}, u32[]{:S(2)}, u32[]{:S(2)}) collective-permute-start(f32[85,128]{1,0:T(8,128)S(1)} %get-tuple-element.20), channel_id=1, source_target_pairs={{0,78},{1,79},{2,80},{3,81},{4,82},{5,83},{6,84},{7,85},{8,86},{9,... | collective-permute-start | bytes 130568 | tf_op jit(solution)/shard_map/ppermute | solution.py:22
  31.9 12.3 %collective-permute-start.3 = (f32[85,128]{1,0:T(8,128)S(1)}, f32[85,128]{1,0:T(8,128)S(1)}, u32[]{:S(2)}, u32[]{:S(2)}) collective-permute-start(f32[85,128]{1,0:T(8,128)S(1)} %get-tuple-element.21), channel_id=1, source_target_pairs={{0,18},{1,19},{2,20},{3,21},{4,22},{5,23},{6,24},{7,25},{8,26},{9,... | collective-permute-start | bytes 130568 | tf_op jit(solution)/shard_map/ppermute | solution.py:22
  44.3 6.5 %collective-permute-start.4 = (f32[17,128]{1,0:T(8,128)S(1)}, f32[17,128]{1,0:T(8,128)S(1)}, u32[]{:S(2)}, u32[]{:S(2)}) collective-permute-start(f32[17,128]{1,0:T(8,128)S(1)} %halo.1), channel_id=1, source_target_pairs={{0,96},{96,192},{192,288},{288,384},{384,480},{480,576},{576,672},... | collective-permute-start | bytes 26120 | tf_op jit(solution)/shard_map/ppermute | solution.py:27

commit v3 on v2

v3 whole, which is shorter than its diff:
```python
import functools

import jax
import jax.numpy as jnp
from jax import lax
from jax.experimental import pallas as pl
from jax.experimental.pallas import tpu as pltpu
from jax.sharding import PartitionSpec as P


SPACING = 90
LANES = 128
KEPT = 1
VMEM = pl.BlockSpec(memory_space=pltpu.VMEM)
SMEM = pl.BlockSpec(memory_space=pltpu.SMEM)
ANY = pl.BlockSpec(memory_space=pl.ANY)
BF16 = jnp.bfloat16
F32 = jnp.float32


def ring(array, by):
    peers = lax.axis_size("azimuth")
    return lax.ppermute(array, "azimuth", [(i, (i + by) % peers) for i in range(peers)])


def next_band(array):
    peers = lax.axis_size("polar")
    return lax.ppermute(array, "polar", [(i, i + 1) for i in range(peers - 1)])


def near(array):
    return pltpu.with_memory_space_constraint(array, pltpu.VMEM)


def halves(a):
    high = a.astype(BF16)
    return high, (a - high.astype(F32)).astype(BF16)


def dot(a, b):
    return jnp.dot(a, b, preferred_element_type=F32)


def dot_t(a, b):
    return lax.dot_general(a, b, (((1,), (1,)), ((), ())), preferred_element_type=F32)


def unpack(out, packed, residual, rows):
    members = 2
    lons, group, cut, rest = rows
    pad = out.shape[0] // members
    full = lons * group
    out[...] = jnp.zeros(out.shape, F32)
    out[0:full, 0:cut] = packed[0:full, 0:cut]
    out[pad : pad + full, 0:cut] = packed[0:full, cut : 2 * cut]
    for m in range(members):
        for n in range(lons):
            at = m * pad + n * group
            lane = n * rest
            out[at : at + group, cut : cut + rest] = packed[
                residual + m * group : residual + (m + 1) * group, lane : lane + rest
            ]


def pack_kernel(x_ref, out_ref):
    members, lons, lat, fields = x_ref.shape
    cut = LANES // 2
    rest = fields - cut
    for m in range(members):
        out_ref[lons + m] = jnp.zeros((lat, LANES), F32)
        for n in range(lons):
            tile = x_ref[m, n]
            out_ref[n, :, m * cut : (m + 1) * cut] = tile[:, 0:cut]
            out_ref[lons + m, :, n * rest : (n + 1) * rest] = tile[:, cut:fields]


def taps_kernel(index_ref, band_ref, kern_ref, near_ref, upper_ref, near_s, upper_s):
    taps, lat, fields = near_s.shape
    outs = lat // 2
    cut = LANES // 2
    rest = fields - cut
    last = index_ref.shape[0] - 1
    first = band_ref[0] * outs
    upper_s[...] = jnp.zeros(upper_s.shape, F32)
    for o in range(outs):
        here = index_ref[first + o]
        after = index_ref[jnp.minimum(first + o + 1, last)]
        for t in range(taps):
            near_s[t, 2 * o : 2 * o + 2, :] = kern_ref[here, t, 1:3, :]
            upper_s[t, 2 * o + 1 : 2 * o + 2, :] = kern_ref[after, t, 0:1, :]
    for src, dst in ((near_s, near_ref), (upper_s, upper_ref)):
        for t in range(taps):
            tile = src[t]
            dst[t, 0] = jnp.concatenate([tile[:, 0:cut]] * 2, axis=1)
            dst[t, 1] = jnp.concatenate([tile[:, cut:fields]] * (LANES // rest), axis=1)


def partial_kernel(x_ref, left_ref, right_ref, near_ref, upper_ref, _, *rest):
    outs, (halo_ref, near_s, upper_s) = rest[:3], rest[3:]
    tiles, lat, lanes = x_ref.shape
    half = lat // 2
    pairs = tiles - 2
    rows = tiles * half
    upper_s[0:lat, :] = jnp.zeros((lat, lanes), F32)
    for s in range(3):
        base = 3 * s
        for i in range(tiles):
            kind = int(i >= pairs)
            three = (left_ref[i], x_ref[i], right_ref[i])
            near = three[0] * near_ref[base, kind]
            upper = three[0] * upper_ref[base, kind]
            for u in (1, 2):
                near = near + three[u] * near_ref[base + u, kind]
                upper = upper + three[u] * upper_ref[base + u, kind]
            near_s[i * lat : (i + 1) * lat, :] = near
            upper_s[(i + 1) * lat : (i + 2) * lat, :] = upper
        even = near_s[pl.ds(0, rows, stride=2), :]
        odd = near_s[pl.ds(1, rows, stride=2), :]
        above = upper_s[pl.ds(lat - 1, rows, stride=2), :]
        place = lax.broadcasted_iota(jnp.int32, above.shape, 0)
        above = jnp.where(place % half == 0, 0.0, above)
        outs[s][...] = even + odd + above
        halo_ref[s * tiles : (s + 1) * tiles, :] = upper_s[pl.ds(2 * lat - 1, tiles, stride=lat), :]


def spans(total, size):
    return [(at, min(size, total - at)) for at in range(0, total, size)]


def in_kernel(mix_ref, in_hbm, mix_h, mix_l, in_h, in_l, in_v, both_s, sems):
    parts = spans(in_v.shape[0], 256)
    copies = fetch([(in_hbm.at[pl.ds(*p), :], in_v.at[pl.ds(*p), :]) for p in parts], sems)
    rows = mix_ref.shape[0]
    pad = both_s.shape[0] // 2
    mh, ml = halves(mix_ref[...])
    mix_h[...], mix_l[...] = mh, ml
    both_s[...] = jnp.zeros(both_s.shape, BF16)
    both_s[0:rows, :] = mh
    both_s[pad : pad + rows, :] = ml
    total = jnp.zeros(in_h.shape, F32)
    for copy, (at, size) in zip(copies, parts):
        copy.wait()
        wh, wl = halves(in_v[at : at + size, :])
        two = dot(both_s[:, at : at + size], wh)
        total = total + (two[0:rows] + two[pad : pad + rows] + dot(both_s[0:rows, at : at + size], wl))
    in_h[...], in_l[...] = halves(total)


def out_kernel(out_hbm, _, *rest):
    pieces, (low_hbm, down_ref, side_ref, out_v, low_v, sems, low_sems) = rest[:-7], rest[-7:]
    depth = low_v.shape[1]
    blocks = out_v.shape[0] // LANES
    parts = list(reversed(spans(out_v.shape[0], LANES)))
    copies = fetch([(out_hbm.at[pl.ds(*p), :], out_v.at[pl.ds(*p), :]) for p in parts], sems)
    stores = []
    for copy, (at, size) in zip(copies, parts):
        copy.wait()
        block = at // LANES
        if block == blocks:
            continue
        high, low = halves(out_v[at : at + size, 0:depth])
        pieces[block][...] = high
        if block < KEPT:
            pieces[blocks + block][...] = low
            continue
        view = pl.ds(at - KEPT * LANES, size)
        low_v[view, :] = low
        store = pltpu.make_async_copy(low_v.at[view, :], low_hbm.at[view, :], low_sems.at[len(stores)])
        store.start()
        stores.append(store)
    down_ref[...] = jnp.transpose(out_v[:, depth:])
    side_ref[...] = out_v[blocks * LANES :, :]
    for store in stores:
        store.wait()


def join_kernel(low_ref, mid_ref, high_ref, halo_ref, _, *outs):
    tiles = halo_ref.shape[0] // 3
    half = low_ref.shape[0] // tiles
    for s, (src, dst) in enumerate(zip((low_ref, mid_ref, high_ref), outs)):
        dst[...] = src[...]
        view = pl.ds(0, tiles, stride=half)
        dst[view, :] = src[view, :] + halo_ref[s * tiles : (s + 1) * tiles, :]


def fetch(pairs, sems):
    copies = [pltpu.make_async_copy(src, dst, sems.at[i]) for i, (src, dst) in enumerate(pairs)]
    for copy in copies:
        copy.start()
    return copies


def stacked(a):
    return jnp.concatenate(halves(a), axis=0)


def product(both, weight, contract):
    rows = both.shape[0] // 2
    total = contract(both, weight)
    return total[:rows] + total[rows:]


def main_kernel(shape, z_ref, a_ref, b_ref, *rest):
    mix_h, mix_l, in_h, in_l, b_in, down, side = rest[:7]
    pieces, rest = rest[7:-10], rest[-10:]
    low_hbm, out_hbm, sum_s, corr_s, both_s, res_s, low_v, out_v, sems, out_sems = rest
    members, lons, half, embed = out_v.shape
    fields = shape
    blocks = embed // LANES
    count, depth = blocks * LANES, low_v.shape[1]
    kept = KEPT * LANES
    parts = [(0, kept)] + [(kept + at, size) for at, size in spans(count - kept, 256)]
    views = [pl.ds(at - kept, size) for at, size in parts[1:]]
    lows = fetch([(low_hbm.at[v, :], low_v.at[v, :]) for v in views], sems)
    rows = corr_s.shape[0]

    @pl.when(lax.axis_index("polar") >= 0)
    def _():
        sum_s[...] = z_ref[...] + a_ref[...] + b_ref[...]
        cut = LANES // 2
        unpack(corr_s, sum_s, lons * half, (lons, half, cut, fields - cut))
        both = stacked(corr_s[:, 0:fields])
        pre = product(both, in_h[...], dot) + dot(both[:rows], in_l[...]) + b_in[...]
        hidden = 0.5 * pre * (1.0 + lax.erf(pre * 0.7071067811865476))
        both_s[...] = stacked(hidden[:, 0:depth])
        mixed = product(both, mix_h[...], dot) + dot(both[:rows], mix_l[...])
        for k in range(down.shape[0]):
            mixed = mixed + hidden[:, depth + k : depth + k + 1] * down[k : k + 1, :]
        res_s[...] = mixed
        last = jnp.sum(hidden[:, 0:depth] * side[:, 0:depth], axis=1, keepdims=True)
        res_s[:, count : count + 1] = mixed[:, count : count + 1] + last

    stores = []
    for k, (at, size) in enumerate(parts):
        first = at // LANES
        held = [pieces[b][...] for b in range(first, first + size // LANES)]
        total = product(both_s[...], jnp.concatenate(held, axis=0), dot_t)
        if at < kept:
            held = [pieces[blocks + b][...] for b in range(first, first + size // LANES)]
            low = jnp.concatenate(held, axis=0)
        else:
            lows[k - 1].wait()
            low = low_v[at - kept : at - kept + size, :]
        res_s[:, at : at + size] += total + dot_t(both_s[0:rows, :], low)
        end = embed if k == len(parts) - 1 else at + size
        for m in range(members):
            for n in range(lons):
                row = m * (rows // members) + n * half
                out_v[m, n, :, at:end] = res_s[row : row + half, at:end]
        lanes = pl.ds(at, end - at)
        store = pltpu.make_async_copy(out_v.at[:, :, :, lanes], out_hbm.at[:, :, :, lanes], out_sems.at[k])
        store.start()
        stores.append(store)
    for store in stores:
        store.wait()


def per_device(state, kernels, kernel_index, w_mix, w_in, b_in, w_out):
    members, lat, fields, lons = state.shape
    half = lat // 2
    tiles = lons + members
    taps = kernels.shape[2]
    embed, ffn = w_in.shape
    step = SPACING // lons
    S, V, DMA = jax.ShapeDtypeStruct, pltpu.VMEM, pltpu.SemaphoreType.DMA

    x = pl.pallas_call(
        pack_kernel,
        out_shape=V((tiles, lat, LANES), F32),
        in_specs=[VMEM],
        out_specs=VMEM,
        name="pack",
    )(jnp.transpose(state, (0, 3, 1, 2)))
    left = ring(x, step)
    right = ring(x, -step)

    band = lax.axis_index("polar").astype(jnp.int32).reshape(1)
    nearby, upper = pl.pallas_call(
        taps_kernel,
        out_shape=[V((taps, 2, lat, LANES), F32)] * 2,
        in_specs=[SMEM, SMEM, VMEM],
        out_specs=[VMEM] * 2,
        scratch_shapes=[V((taps, lat, fields), F32)] * 2,
        name="taps",
    )(kernel_index, band, jnp.transpose(kernels, (0, 2, 1, 3)))
    parts = len(spans(embed, 256))
    mix_h, mix_l, in_h, in_l = pl.pallas_call(
        in_kernel,
        out_shape=[V((fields, embed), BF16)] * 2 + [V((fields, ffn), BF16)] * 2,
        in_specs=[VMEM, ANY],
        out_specs=[VMEM] * 4,
        scratch_shapes=[V((embed, ffn), F32), V((2 * (-(-fields // 16) * 16), embed), BF16), DMA((parts,))],
        name="w_in",
    )(w_mix, w_in)
    bias = b_in.reshape(1, ffn)

    rows = tiles * half
    low, mid, high, halo = pl.pallas_call(
        partial_kernel,
        out_shape=[V((rows, LANES), F32)] * 3 + [V((3 * tiles, LANES), F32)],
        in_specs=[VMEM] * 5 + [ANY],
        out_specs=[VMEM] * 4,
        scratch_shapes=[V((tiles * lat, LANES), F32), V(((tiles + 1) * lat, LANES), F32)],
        name="partial",
    )(near(x), near(left), near(right), near(nearby), near(upper), near(mix_l))
    above = next_band(halo)

    blocks, depth = embed // LANES, ffn // LANES * LANES
    count = blocks * LANES
    fetched = (blocks - KEPT) * LANES
    parts = len(spans(embed, LANES))
    *pieces, low_w, down, side = pl.pallas_call(
        out_kernel,
        out_shape=[V((LANES, depth), BF16)] * (blocks + KEPT)
        + [S((fetched, depth), BF16), V((ffn - depth, embed), F32), V((embed - count, ffn), F32)],
        in_specs=[ANY] * 2,
        out_specs=[VMEM] * (blocks + KEPT) + [ANY, VMEM, VMEM],
        scratch_shapes=[V((embed, ffn), F32), V((fetched, depth), BF16), DMA((parts,)), DMA((parts,))],
        name="w_out",
    )(jnp.transpose(w_out), near(halo))
    low, mid, high = pl.pallas_call(
        join_kernel,
        out_shape=[V((rows, LANES), F32)] * 3,
        in_specs=[VMEM] * 4 + [ANY],
        out_specs=[VMEM] * 3,
        name="join",
    )(near(low), near(mid), near(high), near(above), near(side))
    from_low = ring(low, 3 * step)
    from_high = ring(high, -3 * step)

    pad = members * (-(-lons * half // 16) * 16)
    out = pl.pallas_call(
        functools.partial(main_kernel, fields),
        out_shape=S((members, lons, half, embed), F32),
        in_specs=[VMEM] * (10 + blocks + KEPT) + [ANY],
        out_specs=ANY,
        scratch_shapes=[
            V((rows, LANES), F32),
            V((pad, LANES), F32),
            V((2 * pad, depth), BF16),
            V((pad, embed), F32),
            V((fetched, depth), BF16),
            V((members, lons, half, embed), F32),
            DMA((1 + len(spans(fetched, 256)),)),
            DMA((1 + len(spans(fetched, 256)),)),
        ],
        name="main",
    )(*(near(a) for a in (mid, from_low, from_high, mix_h, mix_l, in_h, in_l, bias, down, side, *pieces)), low_w)
    return jnp.transpose(out, (0, 2, 1, 3))


def solution(mesh):
    placed = (P(None, "polar", None, "azimuth"), P(), P(), P(), P(), P(), P())
    return jax.shard_map(
        per_device,
        mesh=mesh,
        in_specs=placed,
        out_specs=P(None, "polar", "azimuth", None),
        check_vma=False,
    )
```

time: 54.2 us -> 52.2 us (0.963)
  the two profiles are of different devices: /device:TPU:2 before, /device:TPU:20 now
where the time goes in v3:
time: 52.2 us; the launch traced here: 51.9 us
  starting transfers between devices  32.2 us (62%)
  Pallas kernels  11.8 us (23%)
  waiting for transfers between devices  7.79 us (15%)
    ppermute x4, starting transfers between devices, ring(): lax.ppermute(array, 'azimuth', [(i, (i + by) % peers) for i in range(peer...  29.5 us
    ppermute x4, waiting for transfers between devices, ring(): lax.ppermute(array, 'azimuth', [(i, (i + by) % peers) for i in range(peer...  6.51 us
    pallas_call x1, Pallas kernels, per_device(): pl.pallas_call(in_kernel, out_shape=[V((fields, embed), BF16)] * 2 + [V((...  3.48 us
    pallas_call x1, Pallas kernels, per_device(): pl.pallas_call(functools.partial(main_kernel, fields), out_shape=S((membe...  3.18 us
    pallas_call x1, Pallas kernels, per_device(): pl.pallas_call(out_kernel, out_shape=[V((LANES, depth), BF16)] * (blocks...  2.69 us
    ppermute x1, starting transfers between devices, next_band(): return lax.ppermute(array, 'polar', [(i, i + 1) for i in range(peers - 1)])  2.68 us
    pallas_call x1, Pallas kernels, per_device(): pl.pallas_call(taps_kernel, out_shape=[V((taps, 2, lat, LANES), F32)] * 2...  1.29 us
    ppermute x1, waiting for transfers between devices, next_band(): return lax.ppermute(array, 'polar', [(i, i + 1) for i in range(peers - 1)])  1.27 us
  transfers between devices with their start and end apart: 5, of which 3 were waited for; matrix products, arithmetic and copies ran while one was open for 0% of the time, Pallas kernels for 14%

profile of v3, /device:TPU:20, one launch (start us, length us, event | category | flops | bytes accessed | tf_op | source)
XLA Modules:
  0.0 51.9 jit_solution(8734117340874341655)
XLA Ops:
  0.0 1.0 %pack.1.x_ref = f32[17,8,128]{2,1,0:T(8,128)S(1)} custom-call(f32[2,15,8,72]{3,2,1,0:T(8,128)} %bitcast.7), custom_call_target="tpu_custom_call" | custom-call | tf_op jit(solution)/shard_map/pack/pallas_call | solution.py:267
  1.0 17.8 %collective-permute-start.1 = (f32[17,8,128]{2,1,0:T(8,128)S(1)}, f32[17,8,128]{2,1,0:T(8,128)S(1)}, u32[]{:S(2)}, u32[]{:S(2)}) collective-permute-start(f32[17,8,128]{2,1,0:T(8,128)S(1)} %pack.1.x_ref), channel_id=1, source_target_pairs={{0,90},{1,91},{2,92},{3,93},{4,94},{5,95},{6,0},{7,1},{8,2},{9,3},... | collective-permute-start | bytes 208904 | tf_op jit(solution)/shard_map/ppermute | solution.py:23
  18.8 1.9 %collective-permute-start = (f32[17,8,128]{2,1,0:T(8,128)S(1)}, f32[17,8,128]{2,1,0:T(8,128)S(1)}, u32[]{:S(2)}, u32[]{:S(2)}) collective-permute-start(f32[17,8,128]{2,1,0:T(8,128)S(1)} %pack.1.x_ref), channel_id=1, source_target_pairs={{0,6},{1,7},{2,8},{3,9},{4,10},{5,11},{6,12},{7,13},{8,14},{9,15},... | collective-permute-start | bytes 208904 | tf_op jit(solution)/shard_map/ppermute | solution.py:23
  20.8 0.0 copy-start
  20.8 3.5 %w_in.1 = (bf16[72,641]{1,0:T(8,128)(2,1)S(1)}, bf16[72,641]{1,0:T(8,128)(2,1)S(1)}, bf16[72,1282]{1,0:T(8,128)(2,1)S(1)}, bf16[72,1282]{1,0:T(8,128)(2,1)S(1)}) custom-call(f32[72,641]{1,0:T(8,128)} %mix_ref.1, f32[641,1282]{1,0:T(8,128)} %in_hbm.1), custom_call_target="tpu_custom_call" | custom-call | tf_op jit(solution)/shard_map/w_in/pallas_call | solution.py:287
  24.3 1.3 %taps.1 = (f32[9,2,8,128]{3,2,1,0:T(8,128)S(1)}, f32[9,2,8,128]{3,2,1,0:T(8,128)S(1)}) custom-call(s32[32]{0:T(128)} %index_ref.1, s32[1]{0:T(128)} %bitcast.1.band_ref, f32[9,9,3,72]{3,2,1,0:T(4,128)} %bitcast.6), custom_call_target="tpu_custom_call" | custom-call | tf_op jit(solution)/shard_map/taps/pallas_call | solution.py:278
  25.6 0.0 collective-permute-done.1.right_ref
  25.6 4.3 %collective-permute-done.left_ref = f32[17,8,128]{2,1,0:T(8,128)S(1)} collective-permute-done((f32[17,8,128]{2,1,0:T(8,128)S(1)}, f32[17,8,128]{2,1,0:T(8,128)S(1)}, u32[]{:S(2)}, u32[]{:S(2)}) %collective-permute-start) | collective-permute-done | bytes 69664 | tf_op jit(solution)/shard_map/ppermute | solution.py:23
  29.9 0.1 partial.1
  30.0 2.7 %collective-permute-start.2 = (f32[51,128]{1,0:T(8,128)S(1)}, f32[51,128]{1,0:T(8,128)S(1)}, u32[]{:S(2)}, u32[]{:S(2)}) collective-permute-start(f32[51,128]{1,0:T(8,128)S(1)} %get-tuple-element.33._), channel_id=1, source_target_pairs={{0,96},{96,192},{192,288},{288,384},{384,480},{480,576},{576,672},... | collective-permute-start | bytes 78344 | tf_op jit(solution)/shard_map/ppermute | solution.py:28
  32.7 2.7 %w_out.1 = (bf16[128,1280]{1,0:T(8,128)(2,1)S(1)}, bf16[128,1280]{1,0:T(8,128)(2,1)S(1)}, bf16[128,1280]{1,0:T(8,128)(2,1)S(1)}, bf16[128,1280]{1,0:T(8,128)(2,1...) custom-call(f32[641,1282]{1,0:T(8,128)} %bitcast.5, ...), custom_call_target="tpu_custom_call" | custom-call | tf_op jit(solution)/shard_map/w_out/pallas_call | solution.py:312
  35.4 1.3 %collective-permute-done.2.halo_ref = f32[51,128]{1,0:T(8,128)S(1)} collective-permute-done((f32[51,128]{1,0:T(8,128)S(1)}, f32[51,128]{1,0:T(8,128)S(1)}, u32[]{:S(2)}, u32[]{:S(2)}) %collective-permute-start.2) | collective-permute-done | bytes 26144 | tf_op jit(solution)/shard_map/ppermute | solution.py:28
  36.7 1.9 %collective-permute-start.3 = (f32[68,128]{1,0:T(8,128)S(1)}, f32[68,128]{1,0:T(8,128)S(1)}, u32[]{:S(2)}, u32[]{:S(2)}) collective-permute-start(f32[68,128]{1,0:T(8,128)S(1)} %get-tuple-element.36), channel_id=1, source_target_pairs={{0,18},{1,19},{2,20},{3,21},{4,22},{5,23},{6,24},{7,25},{8,26},{9,... | collective-permute-start | bytes 104456 | tf_op jit(solution)/shard_map/ppermute | solution.py:23
  38.6 7.8 %collective-permute-start.4 = (f32[68,128]{1,0:T(8,128)S(1)}, f32[68,128]{1,0:T(8,128)S(1)}, u32[]{:S(2)}, u32[]{:S(2)}) collective-permute-start(f32[68,128]{1,0:T(8,128)S(1)} %get-tuple-element.37), channel_id=1, source_target_pairs={{0,78},{1,79},{2,80},{3,81},{4,82},{5,83},{6,84},{7,85},{8,86},{9,... | collective-permute-start | bytes 104456 | tf_op jit(solution)/shard_map/ppermute | solution.py:23
  46.4 0.0 copy-done
  46.5 0.0 collective-permute-done.3.a_ref
  46.5 2.2 %collective-permute-done.4.b_ref = f32[68,128]{1,0:T(8,128)S(1)} collective-permute-done((f32[68,128]{1,0:T(8,128)S(1)}, f32[68,128]{1,0:T(8,128)S(1)}, u32[]{:S(2)}, u32[]{:S(2)}) %collective-permute-start.4) | collective-permute-done | bytes 34848 | tf_op jit(solution)/shard_map/ppermute | solution.py:23
  48.7 3.2 %main.1 = f32[2,15,4,641]{3,2,1,0:T(4,128)} custom-call(f32[68,128]{1,0:T(8,128)S(1)} %get-tuple-element.35.z_ref, f32[68,128]{1,0:T(8,128)S(1)} %collective-permute-done.3.a_ref, f32[68,128]{1,0:T(8,128)S(1)} %collective-permute-done.4.b_ref, bf16[72,641]{1,0:T(8,128)(2,1)S(1)} %get-tuple-element.38.rest_0_, ...), custom_call_target="tpu_custom_call" | custom-call | tf_op jit(solution)/shard_map/main/pallas_call | solution.py:332
  (2 shorter events, 0.0 us)
Async XLA Ops:
  1.0 24.6 %collective-permute-start.1 = (f32[17,8,128]{2,1,0:T(8,128)S(1)}, f32[17,8,128]{2,1,0:T(8,128)S(1)}, u32[]{:S(2)}, u32[]{:S(2)}) collective-permute-start(f32[17,8,128]{2,1,0:T(8,128)S(1)} %pack.1.x_ref), channel_id=1, source_target_pairs={{0,90},{1,91},{2,92},{3,93},{4,94},{5,95},{6,0},{7,1},{8,2},{9,3},... | collective-permute-start | bytes 208904 | tf_op jit(solution)/shard_map/ppermute | solution.py:23
  18.8 11.0 %collective-permute-start = (f32[17,8,128]{2,1,0:T(8,128)S(1)}, f32[17,8,128]{2,1,0:T(8,128)S(1)}, u32[]{:S(2)}, u32[]{:S(2)}) collective-permute-start(f32[17,8,128]{2,1,0:T(8,128)S(1)} %pack.1.x_ref), channel_id=1, source_target_pairs={{0,6},{1,7},{2,8},{3,9},{4,10},{5,11},{6,12},{7,13},{8,14},{9,15},... | collective-permute-start | bytes 208904 | tf_op jit(solution)/shard_map/ppermute | solution.py:23
  20.8 25.7 %copy-start = (f32[1282]{0:T(1024)S(1)}, f32[1282]{0:T(1024)}, u32[]{:S(2)}) copy-start(f32[1282]{0:T(1024)} %param.12) | copy-start | bytes 15388
  30.0 6.7 %collective-permute-start.2 = (f32[51,128]{1,0:T(8,128)S(1)}, f32[51,128]{1,0:T(8,128)S(1)}, u32[]{:S(2)}, u32[]{:S(2)}) collective-permute-start(f32[51,128]{1,0:T(8,128)S(1)} %get-tuple-element.33._), channel_id=1, source_target_pairs={{0,96},{96,192},{192,288},{288,384},{384,480},{480,576},{576,672},... | collective-permute-start | bytes 78344 | tf_op jit(solution)/shard_map/ppermute | solution.py:28
  36.7 9.8 %collective-permute-start.3 = (f32[68,128]{1,0:T(8,128)S(1)}, f32[68,128]{1,0:T(8,128)S(1)}, u32[]{:S(2)}, u32[]{:S(2)}) collective-permute-start(f32[68,128]{1,0:T(8,128)S(1)} %get-tuple-element.36), channel_id=1, source_target_pairs={{0,18},{1,19},{2,20},{3,21},{4,22},{5,23},{6,24},{7,25},{8,26},{9,... | collective-permute-start | bytes 104456 | tf_op jit(solution)/shard_map/ppermute | solution.py:23
  38.6 10.1 %collective-permute-start.4 = (f32[68,128]{1,0:T(8,128)S(1)}, f32[68,128]{1,0:T(8,128)S(1)}, u32[]{:S(2)}, u32[]{:S(2)}) collective-permute-start(f32[68,128]{1,0:T(8,128)S(1)} %get-tuple-element.37), channel_id=1, source_target_pairs={{0,78},{1,79},{2,80},{3,81},{4,82},{5,83},{6,84},{7,85},{8,86},{9,... | collective-permute-start | bytes 104456 | tf_op jit(solution)/shard_map/ppermute | solution.py:23

commit v4 on v3

v4 whole, which is shorter than its diff:
```python
import functools

import jax
import jax.numpy as jnp
from jax import lax
from jax.experimental import pallas as pl
from jax.experimental.pallas import tpu as pltpu
from jax.sharding import PartitionSpec as P


SPACING = 90
LANES = 128
VMEM = pl.BlockSpec(memory_space=pltpu.VMEM)
SMEM = pl.BlockSpec(memory_space=pltpu.SMEM)
ANY = pl.BlockSpec(memory_space=pl.ANY)
BF16 = jnp.bfloat16
F32 = jnp.float32


call = functools.partial(pl.pallas_call, compiler_params=pltpu.CompilerParams(vmem_limit_bytes=24 << 20))


def ring(array, by):
    peers = lax.axis_size("azimuth")
    return lax.ppermute(array, "azimuth", [(i, (i + by) % peers) for i in range(peers)])


def next_band(array):
    peers = lax.axis_size("polar")
    return lax.ppermute(array, "polar", [(i, i + 1) for i in range(peers - 1)])


def near(array):
    return pltpu.with_memory_space_constraint(array, pltpu.VMEM)


def far(array):
    return pltpu.with_memory_space_constraint(array, pltpu.HBM)


def halves(a):
    high = a.astype(BF16)
    return high, (a - high.astype(F32)).astype(BF16)


def dot(a, b):
    return jnp.dot(a, b, preferred_element_type=F32)


def dot_t(a, b):
    return lax.dot_general(a, b, (((1,), (1,)), ((), ())), preferred_element_type=F32)


def unpack(out, packed, residual, rows):
    members = 2
    lons, group, cut, rest = rows
    pad = out.shape[0] // members
    full = lons * group
    out[...] = jnp.zeros(out.shape, F32)
    out[0:full, 0:cut] = packed[0:full, 0:cut]
    out[pad : pad + full, 0:cut] = packed[0:full, cut : 2 * cut]
    for m in range(members):
        for n in range(lons):
            at = m * pad + n * group
            lane = n * rest
            out[at : at + group, cut : cut + rest] = packed[
                residual + m * group : residual + (m + 1) * group, lane : lane + rest
            ]


def pack_kernel(x_ref, out_ref):
    members, lons, lat, fields = x_ref.shape
    cut = LANES // 2
    rest = fields - cut
    for m in range(members):
        out_ref[lons + m] = jnp.zeros((lat, LANES), F32)
        for n in range(lons):
            tile = x_ref[m, n]
            out_ref[n, :, m * cut : (m + 1) * cut] = tile[:, 0:cut]
            out_ref[lons + m, :, n * rest : (n + 1) * rest] = tile[:, cut:fields]


def taps_kernel(index_ref, kern_ref, near_ref, upper_ref, near_s, upper_s):
    taps, lat, fields = near_s.shape
    outs = lat // 2
    cut = LANES // 2
    rest = fields - cut
    last = index_ref.shape[0] - 1
    first = lax.axis_index("polar") * outs
    upper_s[...] = jnp.zeros(upper_s.shape, F32)
    for o in range(outs):
        here = index_ref[first + o]
        after = index_ref[jnp.minimum(first + o + 1, last)]
        for t in range(taps):
            near_s[t, 2 * o : 2 * o + 2, :] = kern_ref[here, t, 1:3, :]
            upper_s[t, 2 * o + 1 : 2 * o + 2, :] = kern_ref[after, t, 0:1, :]
    for src, dst in ((near_s, near_ref), (upper_s, upper_ref)):
        for t in range(taps):
            tile = src[t]
            dst[t, 0] = jnp.concatenate([tile[:, 0:cut]] * 2, axis=1)
            dst[t, 1] = jnp.concatenate([tile[:, cut:fields]] * (LANES // rest), axis=1)


def partial_kernel(x_ref, left_ref, right_ref, near_ref, upper_ref, _, *rest):
    outs, (halo_ref, near_s, upper_s) = rest[:3], rest[3:]
    tiles, lat, lanes = x_ref.shape
    half = lat // 2
    pairs = tiles - 2
    rows = tiles * half
    upper_s[0:lat, :] = jnp.zeros((lat, lanes), F32)
    for s in range(3):
        base = 3 * s
        for i in range(tiles):
            kind = int(i >= pairs)
            three = (left_ref[i], x_ref[i], right_ref[i])
            near = three[0] * near_ref[base, kind]
            upper = three[0] * upper_ref[base, kind]
            for u in (1, 2):
                near = near + three[u] * near_ref[base + u, kind]
                upper = upper + three[u] * upper_ref[base + u, kind]
            near_s[i * lat : (i + 1) * lat, :] = near
            upper_s[(i + 1) * lat : (i + 2) * lat, :] = upper
        even = near_s[pl.ds(0, rows, stride=2), :]
        odd = near_s[pl.ds(1, rows, stride=2), :]
        above = upper_s[pl.ds(lat - 1, rows, stride=2), :]
        place = lax.broadcasted_iota(jnp.int32, above.shape, 0)
        above = jnp.where(place % half == 0, 0.0, above)
        outs[s][...] = even + odd + above
        halo_ref[s * tiles : (s + 1) * tiles, :] = upper_s[pl.ds(2 * lat - 1, tiles, stride=lat), :]


def in_kernel(mix_ref, in_hbm, mix_s, in_s, both_s, in_v, sems):
    parts = [(at, min(256, in_v.shape[0] - at)) for at in range(0, in_v.shape[0], 256)]
    copies = []
    for k, part in enumerate(parts):
        view = pl.ds(*part)
        copies.append(pltpu.make_async_copy(in_hbm.at[view, :], in_v.at[view, :], sems.at[k]))
        copies[-1].start()
    rows = mix_ref.shape[0]
    pad = both_s.shape[0] // 2
    mh, ml = halves(mix_ref[...])
    for k, part in enumerate((mh, mh, ml)):
        mix_s[k * pad : (k + 1) * pad, :] = jnp.zeros((pad, mix_s.shape[1]), BF16)
        mix_s[k * pad : k * pad + rows, :] = part
    both_s[...] = jnp.zeros(both_s.shape, BF16)
    both_s[0:rows, :] = mh
    both_s[pad : pad + rows, :] = ml
    total = jnp.zeros((pad, in_v.shape[1]), F32)
    for copy, (at, size) in zip(copies, parts):
        copy.wait()
        wh, wl = halves(in_v[at : at + size, :])
        both = both_s[:, at : at + size]
        two = dot(both, wh)
        total = total + (two[0:pad] + two[pad : 2 * pad] + dot(both[0:pad], wl))
    high, low = halves(total)
    for k, part in enumerate((high, high, low)):
        in_s[k * pad : (k + 1) * pad, :] = part


def out_kernel(out_ref, _, out_h, out_l, down_ref, side_ref):
    count, depth = out_h.shape
    out_h[...], out_l[...] = halves(out_ref[0:count, 0:depth])
    down_ref[...] = jnp.transpose(out_ref[:, depth:])
    side_ref[...] = out_ref[count:, :]


def join_kernel(low_ref, mid_ref, high_ref, halo_ref, _, *outs):
    tiles = halo_ref.shape[0] // 3
    half = low_ref.shape[0] // tiles
    for s, (src, dst) in enumerate(zip((low_ref, mid_ref, high_ref), outs)):
        view = pl.ds(0, tiles, stride=half)
        dst[view, :] = src[view, :] + halo_ref[s * tiles : (s + 1) * tiles, :]


def stacked(a):
    return jnp.concatenate(halves(a), axis=0)


def product(both, weight, contract):
    rows = both.shape[0] // 2
    total = contract(both, weight)
    return total[:rows] + total[rows:]


def main_kernel(fields, z_ref, a_ref, b_ref, mix_ref, in_ref, b_in, down, side, out_h, out_l, out_ref, sum_s, corr_s, both_s):
    members, lons, half, _ = out_ref.shape
    count, depth = out_h.shape
    rows = corr_s.shape[0]
    pad = in_ref.shape[0] // 3
    sum_s[...] = z_ref[...] + a_ref[...] + b_ref[...]
    cut = LANES // 2
    unpack(corr_s, sum_s, lons * half, (lons, half, cut, fields - cut))
    high, low = halves(corr_s[:, 0:fields])
    both_s[...] = jnp.zeros(both_s.shape, BF16)
    for k, part in enumerate((high, low, high)):
        both_s[:, k * pad : k * pad + fields] = part
    corr = both_s[:, 0 : 3 * pad]
    pre = dot(corr, in_ref[...]) + b_in[...]
    hidden = 0.5 * pre * (1.0 + lax.erf(pre * 0.7071067811865476))
    both = stacked(hidden[:, 0:depth])
    res = dot(corr, mix_ref[...])
    for k in range(down.shape[0]):
        res = res + hidden[:, depth + k : depth + k + 1] * down[k : k + 1, :]
    last = jnp.sum(hidden[:, 0:depth] * side[:, 0:depth], axis=1, keepdims=True)
    last = res[:, count : count + 1] + last
    res = res[:, 0:count] + product(both, out_h[...], dot_t) + dot_t(both[:rows], out_l[...])
    for m in range(members):
        for n in range(lons):
            row = m * (rows // members) + n * half
            out_ref[m, n, :, 0:count] = res[row : row + half]
            out_ref[m, n, :, count : count + 1] = last[row : row + half]


def per_device(state, kernels, kernel_index, w_mix, w_in, b_in, w_out):
    members, lat, fields, lons = state.shape
    half = lat // 2
    tiles = lons + members
    taps = kernels.shape[2]
    embed, ffn = w_in.shape
    step = SPACING // lons
    S, V = jax.ShapeDtypeStruct, pltpu.VMEM

    x = call(
        pack_kernel,
        out_shape=V((tiles, lat, LANES), F32),
        in_specs=[VMEM],
        out_specs=VMEM,
        name="pack",
    )(far(jnp.transpose(state, (0, 3, 1, 2))))
    left = ring(x, step)
    right = ring(x, -step)

    nearby, upper = call(
        taps_kernel,
        out_shape=[V((taps, 2, lat, LANES), F32)] * 2,
        in_specs=[SMEM, VMEM],
        out_specs=[VMEM] * 2,
        scratch_shapes=[V((taps, lat, fields), F32)] * 2,
        name="taps",
    )(far(kernel_index), far(jnp.transpose(kernels, (0, 2, 1, 3))))
    deep = -(-fields // 16) * 16
    mix_s, in_s = call(
        in_kernel,
        out_shape=[V((3 * deep, embed), BF16), V((3 * deep, ffn), BF16)],
        in_specs=[VMEM, ANY],
        out_specs=[VMEM] * 2,
        scratch_shapes=[V((2 * deep, embed), BF16), V((embed, ffn), F32), pltpu.SemaphoreType.DMA((-(-embed // 256),))],
        name="w_in",
    )(far(w_mix), far(w_in))
    bias = b_in.reshape(1, ffn)

    rows = tiles * half
    low, mid, high, halo = call(
        partial_kernel,
        out_shape=[V((rows, LANES), F32)] * 3 + [V((3 * tiles, LANES), F32)],
        in_specs=[VMEM] * 5 + [ANY],
        out_specs=[VMEM] * 4,
        scratch_shapes=[V((tiles * lat, LANES), F32), V(((tiles + 1) * lat, LANES), F32)],
        name="partial",
    )(near(x), near(left), near(right), near(nearby), near(upper), near(mix_s))
    above = next_band(halo)

    count, depth = embed // LANES * LANES, ffn // LANES * LANES
    out_h, out_l, down, side = call(
        out_kernel,
        out_shape=[V((count, depth), BF16)] * 2 + [V((ffn - depth, embed), F32), V((embed - count, ffn), F32)],
        in_specs=[VMEM, ANY],
        out_specs=[VMEM] * 4,
        name="w_out",
    )(near(jnp.transpose(w_out)), near(halo))
    low, mid, high = call(
        join_kernel,
        out_shape=[V((rows, LANES), F32)] * 3,
        in_specs=[VMEM] * 4 + [ANY],
        out_specs=[VMEM] * 3,
        input_output_aliases={0: 0, 1: 1, 2: 2},
        name="join",
    )(near(low), near(mid), near(high), near(above), near(side))
    from_low = ring(low, 3 * step)
    from_high = ring(high, -3 * step)

    pad = members * (-(-lons * half // 16) * 16)
    out = call(
        functools.partial(main_kernel, fields),
        out_shape=S((members, lons, half, embed), F32),
        in_specs=[VMEM] * 10,
        out_specs=VMEM,
        scratch_shapes=[V((rows, LANES), F32), V((pad, LANES), F32), V((pad, 2 * LANES), BF16)],
        name="main",
    )(*(near(a) for a in (mid, from_low, from_high, mix_s, in_s, bias, down, side, out_h, out_l)))
    return jnp.transpose(out, (0, 2, 1, 3))


def solution(mesh):
    placed = (P(None, "polar", None, "azimuth"), P(), P(), P(), P(), P(), P())
    return jax.shard_map(
        per_device,
        mesh=mesh,
        in_specs=placed,
        out_specs=P(None, "polar", "azimuth", None),
        check_vma=False,
    )
```

time: 52.2 us -> 51 us (0.977)
  the two profiles are of different devices: /device:TPU:20 before, /device:TPU:22 now
where the time goes in v4:
time: 51 us; the launch traced here: 50.8 us
  starting transfers between devices  32.2 us (63%)
  Pallas kernels  9.37 us (18%)
  waiting for transfers between devices  9.11 us (18%)
    ppermute x4, starting transfers between devices, ring(): lax.ppermute(array, 'azimuth', [(i, (i + by) % peers) for i in range(peer...  29.5 us
    ppermute x4, waiting for transfers between devices, ring(): lax.ppermute(array, 'azimuth', [(i, (i + by) % peers) for i in range(peer...  6.19 us
    pallas_call x1, Pallas kernels, per_device(): call(in_kernel, out_shape=[V((3 * deep, embed), BF16), V((3 * deep, ffn),...  3.48 us
    ppermute x1, waiting for transfers between devices, next_band(): return lax.ppermute(array, 'polar', [(i, i + 1) for i in range(peers - 1)])  2.92 us
    ppermute x1, starting transfers between devices, next_band(): return lax.ppermute(array, 'polar', [(i, i + 1) for i in range(peers - 1)])  2.68 us
    pallas_call x1, Pallas kernels, per_device(): call(functools.partial(main_kernel, fields), out_shape=S((members, lons,...  2.28 us
    pallas_call x1, Pallas kernels, per_device(): call(taps_kernel, out_shape=[V((taps, 2, lat, LANES), F32)] * 2, in_specs...  1.3 us
    pallas_call x1, Pallas kernels, per_device(): call(pack_kernel, out_shape=V((tiles, lat, LANES), F32), in_specs=[VMEM],...  1.15 us
  transfers between devices with their start and end apart: 5, of which 3 were waited for; matrix products, arithmetic and copies ran while one was open for 0% of the time, Pallas kernels for 11%

profile of v4, /device:TPU:22, one launch (start us, length us, event | category | flops | bytes accessed | tf_op | source)
XLA Modules:
  0.0 50.8 jit_solution(15996824125888339287)
XLA Ops:
  0.0 0.0 copy-start
  0.0 1.2 %pack.1.x_ref = f32[17,8,128]{2,1,0:T(8,128)S(1)} custom-call(f32[2,15,8,72]{3,2,1,0:T(8,128)} %bitcast.6), custom_call_target="tpu_custom_call" | custom-call | tf_op jit(solution)/shard_map/pack/pallas_call | solution.py:223
  1.2 17.8 %collective-permute-start.1 = (f32[17,8,128]{2,1,0:T(8,128)S(1)}, f32[17,8,128]{2,1,0:T(8,128)S(1)}, u32[]{:S(2)}, u32[]{:S(2)}) collective-permute-start(f32[17,8,128]{2,1,0:T(8,128)S(1)} %pack.1.x_ref), channel_id=1, source_target_pairs={{0,90},{1,91},{2,92},{3,93},{4,94},{5,95},{6,0},{7,1},{8,2},{9,3},... | collective-permute-start | bytes 208904 | tf_op jit(solution)/shard_map/ppermute | solution.py:25
  19.0 1.9 %collective-permute-start = (f32[17,8,128]{2,1,0:T(8,128)S(1)}, f32[17,8,128]{2,1,0:T(8,128)S(1)}, u32[]{:S(2)}, u32[]{:S(2)}) collective-permute-start(f32[17,8,128]{2,1,0:T(8,128)S(1)} %pack.1.x_ref), channel_id=1, source_target_pairs={{0,6},{1,7},{2,8},{3,9},{4,10},{5,11},{6,12},{7,13},{8,14},{9,15},... | collective-permute-start | bytes 208904 | tf_op jit(solution)/shard_map/ppermute | solution.py:25
  20.9 1.3 %taps.1 = (f32[9,2,8,128]{3,2,1,0:T(8,128)S(1)}, f32[9,2,8,128]{3,2,1,0:T(8,128)S(1)}) custom-call(s32[32]{0:T(128)} %index_ref.1, f32[9,9,3,72]{3,2,1,0:T(4,128)} %bitcast.5), custom_call_target="tpu_custom_call" | custom-call | tf_op jit(solution)/shard_map/taps/pallas_call | solution.py:233
  22.2 0.0 copy-start.1
  22.2 3.5 %w_in.1 = (bf16[240,641]{1,0:T(8,128)(2,1)S(1)}, bf16[240,1282]{1,0:T(8,128)(2,1)S(1)}) custom-call(f32[72,641]{1,0:T(8,128)} %mix_ref.1, f32[641,1282]{1,0:T(8,128)} %in_hbm.1), custom_call_target="tpu_custom_call" | custom-call | tf_op jit(solution)/shard_map/w_in/pallas_call | solution.py:242
  25.7 0.0 collective-permute-done.1.right_ref
  25.7 4.3 %collective-permute-done.left_ref = f32[17,8,128]{2,1,0:T(8,128)S(1)} collective-permute-done((f32[17,8,128]{2,1,0:T(8,128)S(1)}, f32[17,8,128]{2,1,0:T(8,128)S(1)}, u32[]{:S(2)}, u32[]{:S(2)}) %collective-permute-start) | collective-permute-done | bytes 69664 | tf_op jit(solution)/shard_map/ppermute | solution.py:25
  30.0 0.1 partial.1
  30.1 2.7 %collective-permute-start.2 = (f32[51,128]{1,0:T(8,128)S(1)}, f32[51,128]{1,0:T(8,128)S(1)}, u32[]{:S(2)}, u32[]{:S(2)}) collective-permute-start(f32[51,128]{1,0:T(8,128)S(1)} %get-tuple-element.26._), channel_id=1, source_target_pairs={{0,96},{96,192},{192,288},{288,384},{384,480},{480,576},{576,672},... | collective-permute-start | bytes 78344 | tf_op jit(solution)/shard_map/ppermute | solution.py:30
  32.8 0.0 copy-done
  32.8 1.0 %w_out.1 = (bf16[640,1280]{1,0:T(8,128)(2,1)S(1)}, bf16[640,1280]{1,0:T(8,128)(2,1)S(1)}, f32[2,641]{1,0:T(2,128)S(1)}, f32[1,1282]{1,0:T(1,128)S(1)}) custom-call(f32[641,1282]{1,0:T(8,128)S(1)} %bitcast.4, f32[51,128]{1,0:T(8,128)S(1)} %get-tuple-element.26._), custom_call_target="tpu_custom_call" | custom-call | tf_op jit(solution)/shard_map/w_out/pallas_call | solution.py:264
  33.9 2.9 %collective-permute-done.2.halo_ref = f32[51,128]{1,0:T(8,128)S(1)} collective-permute-done((f32[51,128]{1,0:T(8,128)S(1)}, f32[51,128]{1,0:T(8,128)S(1)}, u32[]{:S(2)}, u32[]{:S(2)}) %collective-permute-start.2) | collective-permute-done | bytes 26144 | tf_op jit(solution)/shard_map/ppermute | solution.py:30
  36.8 1.9 %collective-permute-start.3 = (f32[68,128]{1,0:T(8,128)S(1)}, f32[68,128]{1,0:T(8,128)S(1)}, u32[]{:S(2)}, u32[]{:S(2)}) collective-permute-start(f32[68,128]{1,0:T(8,128)S(1)} %get-tuple-element.29), channel_id=1, source_target_pairs={{0,18},{1,19},{2,20},{3,21},{4,22},{5,23},{6,24},{7,25},{8,26},{9,... | collective-permute-start | bytes 104456 | tf_op jit(solution)/shard_map/ppermute | solution.py:25
  38.7 7.8 %collective-permute-start.4 = (f32[68,128]{1,0:T(8,128)S(1)}, f32[68,128]{1,0:T(8,128)S(1)}, u32[]{:S(2)}, u32[]{:S(2)}) collective-permute-start(f32[68,128]{1,0:T(8,128)S(1)} %get-tuple-element.30), channel_id=1, source_target_pairs={{0,78},{1,79},{2,80},{3,81},{4,82},{5,83},{6,84},{7,85},{8,86},{9,... | collective-permute-start | bytes 104456 | tf_op jit(solution)/shard_map/ppermute | solution.py:25
  46.6 0.0 copy-done.1
  46.6 0.0 collective-permute-done.3.a_ref
  46.6 1.9 %collective-permute-done.4.b_ref = f32[68,128]{1,0:T(8,128)S(1)} collective-permute-done((f32[68,128]{1,0:T(8,128)S(1)}, f32[68,128]{1,0:T(8,128)S(1)}, u32[]{:S(2)}, u32[]{:S(2)}) %collective-permute-start.4) | collective-permute-done | bytes 34848 | tf_op jit(solution)/shard_map/ppermute | solution.py:25
  48.5 2.3 %main.1 = f32[2,15,4,641]{3,2,1,0:T(4,128)} custom-call(f32[68,128]{1,0:T(8,128)S(1)} %get-tuple-element.28.z_ref, f32[68,128]{1,0:T(8,128)S(1)} %collective-permute-done.3.a_ref, f32[68,128]{1,0:T(8,128)S(1)} %collective-permute-done.4.b_ref, bf16[240,641]{1,0:T(8,128)(2,1)S(1)} %get-tuple-element.22._.mix_ref, ...), custom_call_target="tpu_custom_call" | custom-call | tf_op jit(solution)/shard_map/main/pallas_call | solution.py:283
  (2 shorter events, 0.0 us)
Async XLA Ops:
  0.0 32.8 %copy-start = (f32[1282,641]{0,1:T(8,128)S(1)}, f32[1282,641]{0,1:T(8,128)}, u32[]{:S(2)}) copy-start(f32[1282,641]{0,1:T(8,128)} %param.13) | copy-start | bytes 9861148
  1.2 24.6 %collective-permute-start.1 = (f32[17,8,128]{2,1,0:T(8,128)S(1)}, f32[17,8,128]{2,1,0:T(8,128)S(1)}, u32[]{:S(2)}, u32[]{:S(2)}) collective-permute-start(f32[17,8,128]{2,1,0:T(8,128)S(1)} %pack.1.x_ref), channel_id=1, source_target_pairs={{0,90},{1,91},{2,92},{3,93},{4,94},{5,95},{6,0},{7,1},{8,2},{9,3},... | collective-permute-start | bytes 208904 | tf_op jit(solution)/shard_map/ppermute | solution.py:25
  19.0 11.0 %collective-permute-start = (f32[17,8,128]{2,1,0:T(8,128)S(1)}, f32[17,8,128]{2,1,0:T(8,128)S(1)}, u32[]{:S(2)}, u32[]{:S(2)}) collective-permute-start(f32[17,8,128]{2,1,0:T(8,128)S(1)} %pack.1.x_ref), channel_id=1, source_target_pairs={{0,6},{1,7},{2,8},{3,9},{4,10},{5,11},{6,12},{7,13},{8,14},{9,15},... | collective-permute-start | bytes 208904 | tf_op jit(solution)/shard_map/ppermute | solution.py:25
  22.2 24.4 %copy-start.1 = (f32[1282]{0:T(1024)S(1)}, f32[1282]{0:T(1024)}, u32[]{:S(2)}) copy-start(f32[1282]{0:T(1024)} %param.12) | copy-start | bytes 15388
  30.1 6.7 %collective-permute-start.2 = (f32[51,128]{1,0:T(8,128)S(1)}, f32[51,128]{1,0:T(8,128)S(1)}, u32[]{:S(2)}, u32[]{:S(2)}) collective-permute-start(f32[51,128]{1,0:T(8,128)S(1)} %get-tuple-element.26._), channel_id=1, source_target_pairs={{0,96},{96,192},{192,288},{288,384},{384,480},{480,576},{576,672},... | collective-permute-start | bytes 78344 | tf_op jit(solution)/shard_map/ppermute | solution.py:30
  36.8 9.8 %collective-permute-start.3 = (f32[68,128]{1,0:T(8,128)S(1)}, f32[68,128]{1,0:T(8,128)S(1)}, u32[]{:S(2)}, u32[]{:S(2)}) collective-permute-start(f32[68,128]{1,0:T(8,128)S(1)} %get-tuple-element.29), channel_id=1, source_target_pairs={{0,18},{1,19},{2,20},{3,21},{4,22},{5,23},{6,24},{7,25},{8,26},{9,... | collective-permute-start | bytes 104456 | tf_op jit(solution)/shard_map/ppermute | solution.py:25
  38.7 9.8 %collective-permute-start.4 = (f32[68,128]{1,0:T(8,128)S(1)}, f32[68,128]{1,0:T(8,128)S(1)}, u32[]{:S(2)}, u32[]{:S(2)}) collective-permute-start(f32[68,128]{1,0:T(8,128)S(1)} %get-tuple-element.30), channel_id=1, source_target_pairs={{0,78},{1,79},{2,80},{3,81},{4,82},{5,83},{6,84},{7,85},{8,86},{9,... | collective-permute-start | bytes 104456 | tf_op jit(solution)/shard_map/ppermute | solution.py:25

commit v5 on v4

--- a/solution.py
+++ b/solution.py
@@ -45,10 +45,6 @@
 
 def dot(a, b):
     return jnp.dot(a, b, preferred_element_type=F32)
-
-
-def dot_t(a, b):
-    return lax.dot_general(a, b, (((1,), (1,)), ((), ())), preferred_element_type=F32)
 
 
 def unpack(out, packed, residual, rows):
@@ -158,8 +154,8 @@
 
 
 def out_kernel(out_ref, _, out_h, out_l, down_ref, side_ref):
-    count, depth = out_h.shape
-    out_h[...], out_l[...] = halves(out_ref[0:count, 0:depth])
+    depth, count = out_h.shape
+    out_h[...], out_l[...] = halves(jnp.transpose(out_ref[0:count, 0:depth]))
     down_ref[...] = jnp.transpose(out_ref[:, depth:])
     side_ref[...] = out_ref[count:, :]
 
@@ -182,9 +178,10 @@
     return total[:rows] + total[rows:]
 
 
-def main_kernel(fields, z_ref, a_ref, b_ref, mix_ref, in_ref, b_in, down, side, out_h, out_l, out_ref, sum_s, corr_s, both_s):
-    members, lons, half, _ = out_ref.shape
-    count, depth = out_h.shape
+def main_kernel(fields, z_ref, a_ref, b_ref, mix_ref, in_ref, b_in, down, side, out_h, out_l, out_hbm, *scratch):
+    sum_s, corr_s, both_s, out_v, sems = scratch
+    members, lons, half, embed = out_v.shape
+    depth, count = out_h.shape
     rows = corr_s.shape[0]
     pad = in_ref.shape[0] // 3
     sum_s[...] = z_ref[...] + a_ref[...] + b_ref[...]
@@ -203,12 +200,23 @@
         res = res + hidden[:, depth + k : depth + k + 1] * down[k : k + 1, :]
     last = jnp.sum(hidden[:, 0:depth] * side[:, 0:depth], axis=1, keepdims=True)
     last = res[:, count : count + 1] + last
-    res = res[:, 0:count] + product(both, out_h[...], dot_t) + dot_t(both[:rows], out_l[...])
-    for m in range(members):
-        for n in range(lons):
-            row = m * (rows // members) + n * half
-            out_ref[m, n, :, 0:count] = res[row : row + half]
-            out_ref[m, n, :, count : count + 1] = last[row : row + half]
+    stores = []
+    for k, at in enumerate(range(0, count, 2 * LANES)):
+        end = min(at + 2 * LANES, count)
+        part = res[:, at:end] + product(both, out_h[:, at:end], dot) + dot(both[:rows], out_l[:, at:end])
+        stop = embed if end == count else end
+        for m in range(members):
+            for n in range(lons):
+                row = m * (rows // members) + n * half
+                out_v[m, n, :, at:end] = part[row : row + half]
+                if end == count:
+                    out_v[m, n, :, end:stop] = last[row : row + half]
+        view = pl.ds(at, stop - at)
+        store = pltpu.make_async_copy(out_v.at[:, :, :, view], out_hbm.at[:, :, :, view], sems.at[k])
+        store.start()
+        stores.append(store)
+    for store in stores:
+        store.wait()
 
 
 def per_device(state, kernels, kernel_index, w_mix, w_in, b_in, w_out):
@@ -263,7 +271,7 @@
     count, depth = embed // LANES * LANES, ffn // LANES * LANES
     out_h, out_l, down, side = call(
         out_kernel,
-        out_shape=[V((count, depth), BF16)] * 2 + [V((ffn - depth, embed), F32), V((embed - count, ffn), F32)],
+        out_shape=[V((depth, count), BF16)] * 2 + [V((ffn - depth, embed), F32), V((embed - count, ffn), F32)],
         in_specs=[VMEM, ANY],
         out_specs=[VMEM] * 4,
         name="w_out",
@@ -284,8 +292,14 @@
         functools.partial(main_kernel, fields),
         out_shape=S((members, lons, half, embed), F32),
         in_specs=[VMEM] * 10,
-        out_specs=VMEM,
-        scratch_shapes=[V((rows, LANES), F32), V((pad, LANES), F32), V((pad, 2 * LANES), BF16)],
+        out_specs=ANY,
+        scratch_shapes=[
+            V((rows, LANES), F32),
+            V((pad, LANES), F32),
+            V((pad, 2 * LANES), BF16),
+            V((members, lons, half, embed), F32),
+            pltpu.SemaphoreType.DMA((-(-count // (2 * LANES)),)),
+        ],
         name="main",
     )(*(near(a) for a in (mid, from_low, from_high, mix_s, in_s, bias, down, side, out_h, out_l)))
     return jnp.transpose(out, (0, 2, 1, 3))

time: 51 us -> 50.8 us (level)
  no operation moved by 1% of the time
where the time goes in v5:
time: 50.8 us; the launch traced here: 50.5 us
  starting transfers between devices  32.2 us (63%)
  waiting for transfers between devices  9.19 us (18%)
  Pallas kernels  9.05 us (18%)
    ppermute x4, starting transfers between devices, ring(): lax.ppermute(array, 'azimuth', [(i, (i + by) % peers) for i in range(peer...  29.5 us
    ppermute x4, waiting for transfers between devices, ring(): lax.ppermute(array, 'azimuth', [(i, (i + by) % peers) for i in range(peer...  6.19 us
    pallas_call x1, Pallas kernels, per_device(): call(in_kernel, out_shape=[V((3 * deep, embed), BF16), V((3 * deep, ffn),...  3.48 us
    ppermute x1, waiting for transfers between devices, next_band(): return lax.ppermute(array, 'polar', [(i, i + 1) for i in range(peers - 1)])  3.01 us
    ppermute x1, starting transfers between devices, next_band(): return lax.ppermute(array, 'polar', [(i, i + 1) for i in range(peers - 1)])  2.68 us
    pallas_call x1, Pallas kernels, per_device(): call(functools.partial(main_kernel, fields), out_shape=S((members, lons,...  2.03 us
    pallas_call x1, Pallas kernels, per_device(): call(taps_kernel, out_shape=[V((taps, 2, lat, LANES), F32)] * 2, in_specs...  1.3 us
    pallas_call x1, Pallas kernels, per_device(): call(pack_kernel, out_shape=V((tiles, lat, LANES), F32), in_specs=[VMEM],...  1.15 us
  transfers between devices with their start and end apart: 5, of which 3 were waited for; matrix products, arithmetic and copies ran while one was open for 0% of the time, Pallas kernels for 11%

profile of v5, /device:TPU:22, one launch (start us, length us, event | category | flops | bytes accessed | tf_op | source)
XLA Modules:
  0.0 50.5 jit_solution(13684828869121438738)
XLA Ops:
  0.0 0.0 copy-start
  0.0 1.2 %pack.1.x_ref = f32[17,8,128]{2,1,0:T(8,128)S(1)} custom-call(f32[2,15,8,72]{3,2,1,0:T(8,128)} %bitcast.6), custom_call_target="tpu_custom_call" | custom-call | tf_op jit(solution)/shard_map/pack/pallas_call | solution.py:231
  1.2 17.8 %collective-permute-start.1 = (f32[17,8,128]{2,1,0:T(8,128)S(1)}, f32[17,8,128]{2,1,0:T(8,128)S(1)}, u32[]{:S(2)}, u32[]{:S(2)}) collective-permute-start(f32[17,8,128]{2,1,0:T(8,128)S(1)} %pack.1.x_ref), channel_id=1, source_target_pairs={{0,90},{1,91},{2,92},{3,93},{4,94},{5,95},{6,0},{7,1},{8,2},{9,3},... | collective-permute-start | bytes 208904 | tf_op jit(solution)/shard_map/ppermute | solution.py:25
  19.0 1.9 %collective-permute-start = (f32[17,8,128]{2,1,0:T(8,128)S(1)}, f32[17,8,128]{2,1,0:T(8,128)S(1)}, u32[]{:S(2)}, u32[]{:S(2)}) collective-permute-start(f32[17,8,128]{2,1,0:T(8,128)S(1)} %pack.1.x_ref), channel_id=1, source_target_pairs={{0,6},{1,7},{2,8},{3,9},{4,10},{5,11},{6,12},{7,13},{8,14},{9,15},... | collective-permute-start | bytes 208904 | tf_op jit(solution)/shard_map/ppermute | solution.py:25
  20.9 1.3 %taps.1 = (f32[9,2,8,128]{3,2,1,0:T(8,128)S(1)}, f32[9,2,8,128]{3,2,1,0:T(8,128)S(1)}) custom-call(s32[32]{0:T(128)} %index_ref.1, f32[9,9,3,72]{3,2,1,0:T(4,128)} %bitcast.5), custom_call_target="tpu_custom_call" | custom-call | tf_op jit(solution)/shard_map/taps/pallas_call | solution.py:241
  22.2 0.0 copy-start.1
  22.2 3.5 %w_in.1 = (bf16[240,641]{1,0:T(8,128)(2,1)S(1)}, bf16[240,1282]{1,0:T(8,128)(2,1)S(1)}) custom-call(f32[72,641]{1,0:T(8,128)} %mix_ref.1, f32[641,1282]{1,0:T(8,128)} %in_hbm.1), custom_call_target="tpu_custom_call" | custom-call | tf_op jit(solution)/shard_map/w_in/pallas_call | solution.py:250
  25.7 0.0 collective-permute-done.1.right_ref
  25.7 4.3 %collective-permute-done.left_ref = f32[17,8,128]{2,1,0:T(8,128)S(1)} collective-permute-done((f32[17,8,128]{2,1,0:T(8,128)S(1)}, f32[17,8,128]{2,1,0:T(8,128)S(1)}, u32[]{:S(2)}, u32[]{:S(2)}) %collective-permute-start) | collective-permute-done | bytes 69664 | tf_op jit(solution)/shard_map/ppermute | solution.py:25
  30.0 0.1 partial.1
  30.1 2.7 %collective-permute-start.2 = (f32[51,128]{1,0:T(8,128)S(1)}, f32[51,128]{1,0:T(8,128)S(1)}, u32[]{:S(2)}, u32[]{:S(2)}) collective-permute-start(f32[51,128]{1,0:T(8,128)S(1)} %get-tuple-element.26._), channel_id=1, source_target_pairs={{0,96},{96,192},{192,288},{288,384},{384,480},{480,576},{576,672},... | collective-permute-start | bytes 78344 | tf_op jit(solution)/shard_map/ppermute | solution.py:30
  32.8 0.0 copy-done
  32.8 1.0 %w_out.1 = (bf16[1280,640]{1,0:T(8,128)(2,1)S(1)}, bf16[1280,640]{1,0:T(8,128)(2,1)S(1)}, f32[2,641]{1,0:T(2,128)S(1)}, f32[1,1282]{1,0:T(1,128)S(1)}) custom-call(f32[641,1282]{1,0:T(8,128)S(1)} %bitcast.4, f32[51,128]{1,0:T(8,128)S(1)} %get-tuple-element.26._), custom_call_target="tpu_custom_call" | custom-call | tf_op jit(solution)/shard_map/w_out/pallas_call | solution.py:272
  33.8 3.0 %collective-permute-done.2.halo_ref = f32[51,128]{1,0:T(8,128)S(1)} collective-permute-done((f32[51,128]{1,0:T(8,128)S(1)}, f32[51,128]{1,0:T(8,128)S(1)}, u32[]{:S(2)}, u32[]{:S(2)}) %collective-permute-start.2) | collective-permute-done | bytes 26144 | tf_op jit(solution)/shard_map/ppermute | solution.py:30
  36.8 1.9 %collective-permute-start.3 = (f32[68,128]{1,0:T(8,128)S(1)}, f32[68,128]{1,0:T(8,128)S(1)}, u32[]{:S(2)}, u32[]{:S(2)}) collective-permute-start(f32[68,128]{1,0:T(8,128)S(1)} %get-tuple-element.29), channel_id=1, source_target_pairs={{0,18},{1,19},{2,20},{3,21},{4,22},{5,23},{6,24},{7,25},{8,26},{9,... | collective-permute-start | bytes 104456 | tf_op jit(solution)/shard_map/ppermute | solution.py:25
  38.7 7.8 %collective-permute-start.4 = (f32[68,128]{1,0:T(8,128)S(1)}, f32[68,128]{1,0:T(8,128)S(1)}, u32[]{:S(2)}, u32[]{:S(2)}) collective-permute-start(f32[68,128]{1,0:T(8,128)S(1)} %get-tuple-element.30), channel_id=1, source_target_pairs={{0,78},{1,79},{2,80},{3,81},{4,82},{5,83},{6,84},{7,85},{8,86},{9,... | collective-permute-start | bytes 104456 | tf_op jit(solution)/shard_map/ppermute | solution.py:25
  46.6 0.0 copy-done.1
  46.6 0.0 collective-permute-done.3.a_ref
  46.6 1.9 %collective-permute-done.4.b_ref = f32[68,128]{1,0:T(8,128)S(1)} collective-permute-done((f32[68,128]{1,0:T(8,128)S(1)}, f32[68,128]{1,0:T(8,128)S(1)}, u32[]{:S(2)}, u32[]{:S(2)}) %collective-permute-start.4) | collective-permute-done | bytes 34848 | tf_op jit(solution)/shard_map/ppermute | solution.py:25
  48.5 2.0 %main.1 = f32[2,15,4,641]{3,2,1,0:T(4,128)} custom-call(f32[68,128]{1,0:T(8,128)S(1)} %get-tuple-element.28.z_ref, f32[68,128]{1,0:T(8,128)S(1)} %collective-permute-done.3.a_ref, f32[68,128]{1,0:T(8,128)S(1)} %collective-permute-done.4.b_ref, bf16[240,641]{1,0:T(8,128)(2,1)S(1)} %get-tuple-element.22._.mix_ref, ...), custom_call_target="tpu_custom_call" | custom-call | tf_op jit(solution)/shard_map/main/pallas_call | solution.py:291
  (2 shorter events, 0.0 us)
Async XLA Ops:
  0.0 32.8 %copy-start = (f32[1282,641]{0,1:T(8,128)S(1)}, f32[1282,641]{0,1:T(8,128)}, u32[]{:S(2)}) copy-start(f32[1282,641]{0,1:T(8,128)} %param.13) | copy-start | bytes 9861148
  1.2 24.6 %collective-permute-start.1 = (f32[17,8,128]{2,1,0:T(8,128)S(1)}, f32[17,8,128]{2,1,0:T(8,128)S(1)}, u32[]{:S(2)}, u32[]{:S(2)}) collective-permute-start(f32[17,8,128]{2,1,0:T(8,128)S(1)} %pack.1.x_ref), channel_id=1, source_target_pairs={{0,90},{1,91},{2,92},{3,93},{4,94},{5,95},{6,0},{7,1},{8,2},{9,3},... | collective-permute-start | bytes 208904 | tf_op jit(solution)/shard_map/ppermute | solution.py:25
  19.0 11.0 %collective-permute-start = (f32[17,8,128]{2,1,0:T(8,128)S(1)}, f32[17,8,128]{2,1,0:T(8,128)S(1)}, u32[]{:S(2)}, u32[]{:S(2)}) collective-permute-start(f32[17,8,128]{2,1,0:T(8,128)S(1)} %pack.1.x_ref), channel_id=1, source_target_pairs={{0,6},{1,7},{2,8},{3,9},{4,10},{5,11},{6,12},{7,13},{8,14},{9,15},... | collective-permute-start | bytes 208904 | tf_op jit(solution)/shard_map/ppermute | solution.py:25
  22.2 24.4 %copy-start.1 = (f32[1282]{0:T(1024)S(1)}, f32[1282]{0:T(1024)}, u32[]{:S(2)}) copy-start(f32[1282]{0:T(1024)} %param.12) | copy-start | bytes 15388
  30.1 6.7 %collective-permute-start.2 = (f32[51,128]{1,0:T(8,128)S(1)}, f32[51,128]{1,0:T(8,128)S(1)}, u32[]{:S(2)}, u32[]{:S(2)}) collective-permute-start(f32[51,128]{1,0:T(8,128)S(1)} %get-tuple-element.26._), channel_id=1, source_target_pairs={{0,96},{96,192},{192,288},{288,384},{384,480},{480,576},{576,672},... | collective-permute-start | bytes 78344 | tf_op jit(solution)/shard_map/ppermute | solution.py:30
  36.8 9.8 %collective-permute-start.3 = (f32[68,128]{1,0:T(8,128)S(1)}, f32[68,128]{1,0:T(8,128)S(1)}, u32[]{:S(2)}, u32[]{:S(2)}) collective-permute-start(f32[68,128]{1,0:T(8,128)S(1)} %get-tuple-element.29), channel_id=1, source_target_pairs={{0,18},{1,19},{2,20},{3,21},{4,22},{5,23},{6,24},{7,25},{8,26},{9,... | collective-permute-start | bytes 104456 | tf_op jit(solution)/shard_map/ppermute | solution.py:25
  38.7 9.8 %collective-permute-start.4 = (f32[68,128]{1,0:T(8,128)S(1)}, f32[68,128]{1,0:T(8,128)S(1)}, u32[]{:S(2)}, u32[]{:S(2)}) collective-permute-start(f32[68,128]{1,0:T(8,128)S(1)} %get-tuple-element.30), channel_id=1, source_target_pairs={{0,78},{1,79},{2,80},{3,81},{4,82},{5,83},{6,84},{7,85},{8,86},{9,... | collective-permute-start | bytes 104456 | tf_op jit(solution)/shard_map/ppermute | solution.py:25
